TPU v7x, 32 devices: a whole 2x2x4 slice. The times are simulated.
32 devices in a mesh: narrow: 4 (over z), wide: 8 (over y, x, core).
Axes of the slice: x: 2, y: 2, z: 4, core: 2. Of those that a mesh axis runs over, the one named last changes fastest.
Arguments:
- layer_input: bfloat16 [32, 512, 640], P(('narrow', 'wide')), may hold values from -6 to 6
- segments: int32 [32, 512], P(('narrow', 'wide')), may hold values from 0 to 7, never falling along the last dimension, each value on 1 to 192 neighbouring positions
- targets: int32 [32, 512], P(('narrow', 'wide')), may hold values from 0 to 24
- loss_mask: int32 [32, 512], P(('narrow', 'wide')), may hold values from 0 to 1
- readout: bfloat16 [640, 25], replicated, may hold values from -0.29882812 to 0.29882812
- attend_gain: bfloat16 [640], P('wide'), may hold values from 0.5 to 1.5
- attend_shift: bfloat16 [640], P('wide'), may hold values from -1.1953125 to 1.1953125
- heads_weight: bfloat16 [640, 1920], P('wide'), may hold values from -0.25 to 0.25
- query_bias: bfloat16 [640], P('wide'), may hold values from -1.1953125 to 1.1953125
- value_bias: bfloat16 [640], P('wide'), may hold values from -1.1953125 to 1.1953125
- output_weight: bfloat16 [640, 640], P('wide'), may hold values from -1.25 to 1.25
- output_bias: bfloat16 [640], P('wide'), may hold values from -1.1953125 to 1.1953125
- forward_gain: bfloat16 [640], P('wide'), may hold values from 0.5 to 1.5
- forward_shift: bfloat16 [640], P('wide'), may hold values from -1.1953125 to 1.1953125
- up_weight: bfloat16 [640, 5120], P('wide'), may hold values from -0.25 to 0.25
- up_bias: bfloat16 [5120], P('wide'), may hold values from -1.1953125 to 1.1953125
- down_weight: bfloat16 [5120, 640], P('wide'), may hold values from -0.125 to 0.125
- down_bias: bfloat16 [640], P('wide'), may hold values from -1.1953125 to 1.1953125
Outputs:
- layer_output: bfloat16 [32, 512, 640], P(('narrow', 'wide'))
- input_grad: float32 [32, 512, 640], P(('narrow', 'wide'))
- attend_gain_grad: float32 [640], P('wide')
- attend_shift_grad: float32 [640], P('wide')
- heads_weight_grad: float32 [640, 1920], P('wide')
- query_bias_grad: float32 [640], P('wide')
- value_bias_grad: float32 [640], P('wide')
- output_weight_grad: float32 [640, 640], P('wide')
- output_bias_grad: float32 [640], P('wide')
- forward_gain_grad: float32 [640], P('wide')
- forward_shift_grad: float32 [640], P('wide')
- up_weight_grad: float32 [640, 5120], P('wide')
- up_bias_grad: float32 [5120], P('wide')
- down_weight_grad: float32 [5120, 640], P('wide')
- down_bias_grad: float32 [640], P('wide')
- loss_sum: float32 [], replicated
- token_count: int32 [], replicated
All inputs are finite; a program needn't handle non-finite values.
Results may differ from a plain program's by a relative error of at most 0.013.
Values may be sent and summed in bfloat16 or wider, within the bound.
No kernel may reach another device: no remote copies, remote signals or barrier semaphores. Data moves between devices by JAX's collectives and lax.ppermute only.
A program may use at most 192 MiB of HBM per device.

v0:
```python
import functools
import math

import jax
import jax.numpy as jnp
from jax import lax
from jax.experimental import pallas as pl
from jax.experimental.pallas import tpu as pltpu
from jax.sharding import PartitionSpec as P

HEADS = 20
HEAD_DIM = 32
LANES = 128
SUBLANES = 8
SEGMENTS = 8
REACH = 192
CHUNK = 256
ROWS = 128
SCALE = 1.0 / math.sqrt(HEAD_DIM)
SCALE2 = math.log2(math.e) * SCALE
F32 = jnp.float32
BF16 = jnp.bfloat16
VECTORS = 8
ATTEND_GAIN, ATTEND_SHIFT, QUERY_BIAS, VALUE_BIAS = 0, 1, 2, 3
OUTPUT_BIAS, FORWARD_GAIN, FORWARD_SHIFT, DOWN_BIAS = 4, 5, 6, 7


def nn(left, right):
    return lax.dot_general(left, right, (((1,), (0,)), ((), ())), preferred_element_type=F32)


def nt(left, right):
    return lax.dot_general(left, right, (((1,), (1,)), ((), ())), preferred_element_type=F32)


def tn(left, right):
    return lax.dot_general(left, right, (((0,), (0,)), ((), ())), preferred_element_type=F32)


def call(kernel, outs, args, positions=None, grid=None, in_specs=None, out_specs=None, scratch=(),
         mib=16, aliases=None):
    whole = pl.BlockSpec(memory_space=pltpu.VMEM)
    in_specs = in_specs or [whole] * len(args)
    args = [
        pltpu.with_memory_space_constraint(arg, pltpu.HBM)
        if spec.memory_space == pltpu.HBM
        else arg
        for arg, spec in zip(args, in_specs)
    ]
    out_specs = out_specs or [whole] * len(outs)
    shapes = [
        pltpu.HBM(*out) if spec.memory_space == pltpu.HBM else jax.ShapeDtypeStruct(*out)
        for out, spec in zip(outs, out_specs)
    ]
    extra = [] if positions is None else [positions]
    return pl.pallas_call(
        kernel,
        out_shape=shapes,
        grid_spec=pltpu.PrefetchScalarGridSpec(
            num_scalar_prefetch=len(extra),
            grid=grid or (),
            in_specs=in_specs,
            out_specs=out_specs,
            scratch_shapes=list(scratch),
        ),
        compiler_params=pltpu.CompilerParams(vmem_limit_bytes=mib * 1024 * 1024),
        input_output_aliases=aliases or {},
        cost_estimate=pl.CostEstimate(flops=1, bytes_accessed=1, transcendentals=0),
    )(*extra, *args)


def unit(values):
    centred = values - jnp.mean(values, axis=-1, keepdims=True)
    spread = jnp.mean(centred * centred, axis=-1, keepdims=True)
    inverse = lax.rsqrt(spread + 1e-05)
    return centred * inverse, inverse


def unit_back(grad, normal, inverse, gain):
    scaled = grad * gain
    mean = jnp.mean(scaled, axis=-1, keepdims=True)
    along = jnp.mean(scaled * normal, axis=-1, keepdims=True)
    return inverse * (scaled - mean - normal * along)


def spans(length):
    chunk = min(CHUNK, length)
    return [
        (at, at + chunk, max(0, at - REACH), min(length, at + chunk + REACH))
        for at in range(0, length, chunk)
    ]


def split3(values):
    first = values.astype(BF16).astype(F32)
    rest = values - first
    second = rest.astype(BF16).astype(F32)
    return [first, second, rest - second]


def key_marks(segment_row):
    at = lax.broadcasted_iota(jnp.int32, (LANES, segment_row.shape[1]), 0)
    ones = (at >= SEGMENTS) & (at < SEGMENTS + 3)
    return jnp.where((at == segment_row) | ones, 1.0, 0.0).astype(BF16).T


def query_marks(segment_row):
    row = lax.broadcasted_iota(jnp.int32, (SEGMENTS, segment_row.shape[1]), 0)
    return jnp.where(row == segment_row, 0.0, -1e30)


def place(rows, head, marks):
    count = rows.shape[1]
    parts = [rows, marks, jnp.zeros((LANES - marks.shape[0], count), BF16)]
    if head < LANES // HEAD_DIM - 1:
        parts.insert(1, jnp.zeros((LANES - HEAD_DIM * (head + 1), count), BF16))
    if head:
        parts.insert(0, jnp.zeros((HEAD_DIM * head, count), BF16))
    return jnp.concatenate(parts, axis=0)


def attend_kernel(row_ref, q_ref, k_ref, v_ref, out_ref, across_ref, lse_ref, marks_ref):
    @pl.when(pl.program_id(0) == 0)
    def _():
        marks_ref[...] = key_marks(row_ref[...])

    length = q_ref.shape[0]
    heads = LANES // HEAD_DIM
    queries = q_ref[...].T
    values = v_ref[...].T
    keys = jnp.concatenate([k_ref[...], marks_ref[...]], axis=1)
    blank = jnp.zeros((SUBLANES, length), F32)
    marks = jnp.concatenate([query_marks(row_ref[...]), blank], axis=0).astype(BF16)
    ones = jnp.ones((SUBLANES, length), BF16)
    bodies = [(head, span) for head in range(heads) for span in spans(length)]

    def rows(head):
        return slice(HEAD_DIM * head, HEAD_DIM * (head + 1))

    summed = [jnp.concatenate([values[rows(head)], ones], axis=0) for head in range(heads)]

    def score(head, span):
        begin, end, low, high = span
        return nn(keys[low:high], place(queries[rows(head), begin:end], head, marks[:, begin:end]))

    def finish(head, span, top, probs):
        begin, end, low, high = span
        out = nn(summed[head][:, low:high], probs)
        total = out[HEAD_DIM : HEAD_DIM + 1]
        across_ref[rows(head), begin:end] = out[:HEAD_DIM] * (1.0 / total)
        lse_ref[head : head + 1, begin:end] = (top + jnp.log2(total)) * (1.0 / SCALE2)

    scores = [score(*body) for body in bodies[:2]]
    waiting = None
    for at, body in enumerate(bodies):
        current = scores.pop(0)
        if at + 2 < len(bodies):
            scores.append(score(*bodies[at + 2]))
        top = jnp.max(current, axis=0, keepdims=True) * SCALE2
        probs = jnp.exp2(current * SCALE2 - top).astype(BF16)
        if waiting is not None:
            finish(*waiting)
        waiting = (*body, top, probs)
    finish(*waiting)
    lse_ref[heads:, :] = jnp.zeros((SUBLANES - heads, length), F32)
    out_ref[...] = across_ref[...].T.astype(BF16)


def attend_back_kernel(
    row_ref, q_ref, k_ref, v_ref, grad_ref, across_ref, lse_ref,
    gq_ref, gk_ref, gv_ref, marks_ref, turned_ref,
):
    @pl.when(pl.program_id(0) == 0)
    def _():
        marks_ref[...] = key_marks(row_ref[...])

    length = q_ref.shape[0]
    grad = grad_ref[...]
    queries = q_ref[...].T
    turned_keys = k_ref[...].T
    grads = grad.T
    keys = jnp.concatenate([k_ref[...], marks_ref[...]], axis=1)
    values = jnp.concatenate([v_ref[...], marks_ref[...]], axis=1)
    low_marks = query_marks(row_ref[...])
    blank = jnp.zeros((SUBLANES, length), F32)
    lane = lax.broadcasted_iota(jnp.int32, (1, LANES), 1) // HEAD_DIM
    heads = []
    for head in range(LANES // HEAD_DIM):
        rows = slice(HEAD_DIM * head, HEAD_DIM * (head + 1))
        inner = jnp.sum(grads[rows].astype(F32) * across_ref[rows, :], axis=0, keepdims=True)
        lse = lse_ref[head : head + 1, :]
        score_marks = jnp.concatenate([low_marks, *split3(-lse), blank[:5]], axis=0)
        inner_marks = jnp.concatenate([blank, *split3(-inner), blank[:5]], axis=0)
        zero = jnp.zeros_like(grad)
        heads.append(
            (
                rows,
                score_marks.astype(BF16),
                inner_marks.astype(BF16),
                jnp.where(lane == head, q_ref[...], zero),
                jnp.where(lane == head, grad, zero),
            )
        )
    bodies = [
        (head, at, span) for head in range(len(heads)) for at, span in enumerate(spans(length))
    ]
    sums = [[None, None] for _ in spans(length)]

    def pair(head, at, span):
        begin, end, low, high = span
        rows, score_marks, inner_marks, _, _ = heads[head]
        return (
            nn(keys[low:high], place(queries[rows, begin:end], head, score_marks[:, begin:end])),
            nn(values[low:high], place(grads[rows, begin:end], head, inner_marks[:, begin:end])),
        )

    def finish(head, at, span, score_grads, probs):
        begin, end, low, high = span
        rows, _, _, own_queries, own_grads = heads[head]
        for which, (left, right) in enumerate(
            ((score_grads, own_queries[begin:end]), (probs, own_grads[begin:end]))
        ):
            part = nn(left, right)
            sums[at][which] = part if sums[at][which] is None else sums[at][which] + part
        turned_ref[rows, begin:end] = nn(turned_keys[rows, low:high], score_grads)

    ahead = [pair(*bodies[0])]
    waiting = None
    for at, body in enumerate(bodies):
        scores, differences = ahead.pop(0)
        if at + 1 < len(bodies):
            ahead.append(pair(*bodies[at + 1]))
        probs = jnp.exp2(scores * SCALE2)
        score_grads = (probs * differences).astype(BF16)
        if waiting is not None:
            finish(*waiting)
        waiting = (*body, score_grads, probs.astype(BF16))
    finish(*waiting)
    gq_ref[...] = (turned_ref[...].T * SCALE).astype(BF16)
    for which, (ref, factor) in enumerate(((gk_ref, SCALE), (gv_ref, 1.0))):
        total = None
        for at, (_, _, low, high) in enumerate(spans(length)):
            parts = [sums[at][which]]
            if low:
                parts.insert(0, jnp.zeros((low, LANES), F32))
            if high < length:
                parts.append(jnp.zeros((length - high, LANES), F32))
            part = jnp.concatenate(parts, axis=0) if len(parts) > 1 else parts[0]
            total = part if total is None else total + part
        ref[...] = (total * factor).astype(BF16)


def attention_specs(length, width, begin=0):
    tiles = width // LANES

    def tile(at, begin=begin):
        return pl.BlockSpec((length, LANES), lambda i: (0, at + begin + i))

    return (
        tiles,
        tile,
        pl.BlockSpec((1, length), lambda i: (0, 0)),
        pl.BlockSpec((LANES, length), lambda i: (begin + i, 0)),
        pl.BlockSpec((SUBLANES, length), lambda i: (begin + i, 0)),
    )


def attend(joined, row):
    length = joined.shape[0]
    width = joined.shape[1] // 3
    tiles, tile, row_spec, across_spec, lse_spec = attention_specs(length, width)
    return call(
        attend_kernel,
        [((length, width), BF16), ((width, length), F32), ((SUBLANES * tiles, length), F32)],
        (row, joined, joined, joined),
        grid=(tiles,),
        in_specs=[row_spec, tile(0), tile(tiles), tile(2 * tiles)],
        out_specs=[tile(0), across_spec, lse_spec],
        scratch=[pltpu.VMEM((length, LANES), BF16)],
    )


def attend_back(joined, row, grad, across, lse, begin=0, end=None):
    length = joined.shape[0]
    width = joined.shape[1] // 3
    specs = attention_specs(length, width, begin)
    tiles, tile, row_spec, across_spec, lse_spec = specs
    count = (end or tiles) - begin
    return call(
        attend_back_kernel,
        [((length, count * LANES), BF16)] * 3,
        (row, joined, joined, joined, grad, across, lse),
        grid=(count,),
        in_specs=[row_spec, tile(0), tile(tiles), tile(2 * tiles), tile(0), across_spec, lse_spec],
        out_specs=[tile(0, 0)] * 3,
        scratch=[pltpu.VMEM((length, LANES), BF16), pltpu.VMEM((LANES, length), F32)],
        mib=24,
    )


def slab_kernel(heads_ref, out_ref, short_ref, up_ref, slab_ref):
    rows = heads_ref.shape[0]
    width = out_ref.shape[1]
    slab_ref[:rows, : 3 * width] = heads_ref[...]
    slab_ref[:rows, 3 * width :] = out_ref[...]
    slab_ref[rows:, :] = jnp.zeros((VECTORS, 4 * width), BF16)
    slab_ref[rows:, :rows] = short_ref[...]
    slab_ref[rows:, LANES : LANES + up_ref.shape[1]] = jnp.broadcast_to(
        up_ref[...], (VECTORS, up_ref.shape[1])
    )


def project_kernel(count, rows, hidden, position_ref, x_ref, *refs):
    slabs, refs = refs[:count], refs[count:]
    length, width = x_ref.shape
    if count:
        low_ref, joined_ref, heads_ref, out_ref, vector_ref, bias_ref, short_ref, sems = refs
        copies = []
        for at, slab in enumerate(slabs):
            begin = pl.multiple_of(position_ref[at] * rows, SUBLANES)
            here = pl.ds(begin, rows)
            for which, (source, target) in enumerate(
                (
                    (slab.at[pl.ds(0, rows), pl.ds(0, 3 * width)], heads_ref.at[here]),
                    (slab.at[pl.ds(0, rows), pl.ds(3 * width, width)], out_ref.at[here]),
                    (slab.at[pl.ds(rows, VECTORS), pl.ds(0, LANES + hidden)], short_ref.at[at]),
                )
            ):
                copy = pltpu.make_async_copy(source, target, sems.at[at, which])
                copy.start()
                copies.append(copy)
    else:
        heads_ref, vector_ref, low_ref, joined_ref = refs
    if count:
        for copy in copies:
            copy.wait()
        vectors = jnp.zeros((VECTORS, width), F32)
        for at in range(count):
            begin = position_ref[at] * rows
            short = short_ref[at, :, :LANES].astype(F32)
            lane = lax.broadcasted_iota(jnp.int32, short.shape, 1)
            short = jnp.where(lane < rows, short, 0.0)
            short = jnp.concatenate([short, jnp.zeros((VECTORS, width - LANES), F32)], axis=1)
            vectors = vectors + pltpu.roll(short, begin, 1)
            if at < count // 2:
                begin = pl.multiple_of(lax.div(position_ref[at], 2) * hidden, LANES)
                bias_ref[:, pl.ds(begin, hidden)] = short_ref[at, :, LANES:].astype(F32)
        vector_ref[...] = vectors
    zero = jnp.zeros((1, width), F32)
    vector = vector_ref[...]
    bias = jnp.concatenate(
        [vector[QUERY_BIAS : QUERY_BIAS + 1], zero, vector[VALUE_BIAS : VALUE_BIAS + 1]], axis=1
    )
    for at in range(0, length, ROWS):
        normal, _ = unit(x_ref[at : at + ROWS, :].astype(F32))
        low_ref[at : at + ROWS, :] = (
            normal * vector[ATTEND_GAIN : ATTEND_GAIN + 1]
            + vector[ATTEND_SHIFT : ATTEND_SHIFT + 1]
        ).astype(BF16)
    for at in range(0, 3 * width, width):
        here = slice(at, at + width)
        joined_ref[:, here] = (nn(low_ref[...], heads_ref[:, here]) + bias[:, here]).astype(BF16)


def middle_kernel(x_ref, attended_ref, out_ref, vector_ref, middle_ref, low_ref):
    vector = vector_ref[...]
    for at in range(0, x_ref.shape[0], ROWS):
        here = slice(at, at + ROWS)
        middle = (
            x_ref[here, :].astype(F32)
            + nn(attended_ref[here, :], out_ref[...])
            + vector[OUTPUT_BIAS : OUTPUT_BIAS + 1]
        )
        middle_ref[here, :] = middle
        normal, _ = unit(middle)
        low_ref[here, :] = (
            normal * vector[FORWARD_GAIN : FORWARD_GAIN + 1]
            + vector[FORWARD_SHIFT : FORWARD_SHIFT + 1]
        ).astype(BF16)


def up_kernel(position_ref, own_ref, other_ref, bias_ref, *refs):
    parts, (act_ref, slope_ref, full_ref) = refs[: len(refs) - 3], refs[len(refs) - 3 :]
    for at, part in enumerate(parts):
        rows = part.shape[0]
        begin = pl.multiple_of(position_ref[at] * rows, SUBLANES)
        full_ref[pl.ds(begin, rows), :] = part[...]
    weight = full_ref[...]
    bias = bias_ref[:1, :]
    length = own_ref.shape[0]
    for which, ref in enumerate((own_ref, other_ref)):
        for at in range(0, length, ROWS):
            upward = nn(ref[at : at + ROWS, :], weight) + bias
            share = 0.5 + 0.5 * lax.erf(upward * math.sqrt(0.5))
            bell = jnp.exp2((upward * upward) * (-0.5 * math.log2(math.e)))
            here = slice(which * length + at, which * length + at + ROWS)
            act_ref[here, :] = (upward * share).astype(BF16)
            slope = share + upward * (bell * (1.0 / math.sqrt(2.0 * math.pi)))
            slope_ref[here, :] = slope.astype(BF16)


def column_specs(half, block):
    block = min(block, half)

    def column(height):
        return pl.BlockSpec((height, block), lambda i, at: (0, i))

    return half // block, block, column


def whole_spec(shape):
    return pl.BlockSpec(shape, lambda i, at: (0,) * len(shape))


def up_project(own, other, bias, parts, positions, hidden):
    length, width = own.shape
    half = bias.shape[1]
    paired = parts[0].shape[1] > half
    steps, block, column = column_specs(half, hidden if paired else 512)
    whole = whole_spec((length, width))

    def part_spec(part):
        if paired:
            return pl.BlockSpec((part.shape[0], block), lambda i, at: (0, 2 * i + at[len(parts)]))
        return column(part.shape[0])

    return call(
        up_kernel,
        [((2 * length, half), BF16), ((2 * length, half), BF16), ((width, half), BF16)],
        (own, other, bias, *parts),
        positions,
        grid=(steps,),
        in_specs=[whole, whole, column(bias.shape[0])] + [part_spec(part) for part in parts],
        out_specs=[column(2 * length), column(2 * length), column(width)],
    )


def down_kernel(position_ref, act_ref, *refs):
    parts, (own_ref, other_ref, full_ref) = refs[: len(refs) - 3], refs[len(refs) - 3 :]
    length = own_ref.shape[0]
    for at, part in enumerate(parts):
        rows = part.shape[0]
        begin = pl.multiple_of(position_ref[at] * rows, SUBLANES)
        full_ref[pl.ds(begin, rows), :] = part[...]
    for which, ref in enumerate((own_ref, other_ref)):
        here = slice(which * length, (which + 1) * length)
        ref[...] = nn(act_ref[here, :], full_ref[...]).astype(ref.dtype)


def down_project(act, parts, positions):
    length = act.shape[0] // 2
    half = act.shape[1]
    width = parts[0].shape[1]
    return call(
        down_kernel,
        [((length, width), F32), ((length, width), BF16), ((half, width), BF16)],
        (act, *parts),
        positions,
        mib=20,
    )


def down_near_kernel(position_ref, act_ref, *refs):
    parts, (sum_ref, full_ref) = refs[:-2], refs[-2:]
    size = parts[0].shape[0]
    for at, part in enumerate(parts):
        rows = part.shape[0]
        begin = pl.multiple_of(position_ref[at] * rows, SUBLANES)
        full_ref[pl.ds(begin, rows), :] = part[...]
    chips = [position_ref[0], lax.div(position_ref[1], 2), lax.div(position_ref[3], 2)]
    length = act_ref.shape[0] // 2
    for which in range(2):
        here = slice(which * length, (which + 1) * length)
        total = None
        for chip in chips:
            units = pl.ds(pl.multiple_of(chip * size, LANES), size)
            part = nn(act_ref[here, units], full_ref[units, :])
            total = part if total is None else total + part
        sum_ref[here, :] = total


def down_far_kernel(position_ref, act_ref, sum_ref, upper_ref, lower_ref, _, own_ref, other_ref, full_ref):
    rows, length = upper_ref.shape[0], own_ref.shape[0]
    size = 2 * rows
    units = pl.ds(pl.multiple_of(lax.div(position_ref[5], 2) * size, LANES), size)
    weight = jnp.concatenate([upper_ref[...], lower_ref[...]], axis=0)
    full_ref[units, :] = weight
    for which, ref in enumerate((own_ref, other_ref)):
        here = slice(which * length, (which + 1) * length)
        ref[...] = (sum_ref[here, :] + nn(act_ref[here, units], weight)).astype(ref.dtype)


def down_project_square(act, near, far, positions):
    length, half, width = act.shape[0] // 2, act.shape[1], near[0].shape[1]
    total, full = call(
        down_near_kernel,
        [((2 * length, width), F32), ((half, width), BF16)],
        (act, *near),
        positions,
        mib=24,
    )
    far = far(total)
    return call(
        down_far_kernel,
        [((length, width), F32), ((length, width), BF16), ((half, width), BF16)],
        (act, total, *far, full),
        positions,
        mib=24,
        aliases={5: 2},
    )


def loss_kernel(
    middle_ref, own_ref, got_ref, vector_ref, readout_ref, target_ref, mask_ref,
    low_ref, down_ref, grad_ref, sums_ref,
):
    result = (
        middle_ref[...]
        + (own_ref[...] + got_ref[...].astype(F32))
        + vector_ref[DOWN_BIAS : DOWN_BIAS + 1, :]
    ).astype(BF16)
    low_ref[...] = result
    logits = nt(readout_ref[...], result)
    length = logits.shape[1]
    top = jnp.max(logits, axis=0, keepdims=True)
    shifted = jnp.exp(logits - top)
    total = jnp.sum(shifted, axis=0, keepdims=True)
    onehot = lax.broadcasted_iota(jnp.int32, logits.shape, 0) == target_ref[...]
    picked = jnp.sum(jnp.where(onehot, logits, 0.0), axis=0, keepdims=True)
    weight = mask_ref[...].astype(F32)
    loss = (top + jnp.log(total) - picked) * weight
    loss_lanes = jnp.zeros((1, LANES), F32)
    count_lanes = jnp.zeros((1, LANES), F32)
    for at in range(0, length, LANES):
        loss_lanes = loss_lanes + loss[:, at : at + LANES]
        count_lanes = count_lanes + weight[:, at : at + LANES]
    lanes = jnp.concatenate([loss_lanes, count_lanes], axis=0)
    lanes = jnp.concatenate([lanes, jnp.zeros((2, result.shape[1] - LANES), F32)], axis=1)
    grad_logits = (weight * (shifted / total - onehot.astype(F32))).astype(BF16)
    grad_ref[...] = grad_logits
    low = tn(grad_logits, readout_ref[...]).astype(BF16)
    down_ref[...] = low
    sums = jnp.sum(low.astype(F32), axis=0, keepdims=True)
    blank = jnp.zeros((SUBLANES - 3, result.shape[1]), F32)
    sums_ref[...] = jnp.concatenate([lanes, sums, blank], axis=0)


def down_grad_kernel(chips, position_ref, act_ref, own_ref, other_ref, *out_refs):
    length = own_ref.shape[0]
    hidden = act_ref.shape[1] // chips
    for offset in range(chips):
        if len(out_refs) == 1:
            begin = offset * hidden
        else:
            begin = pl.multiple_of((position_ref[0] ^ offset) * hidden, LANES)
        here = pl.ds(begin, hidden)
        part = tn(act_ref[:length, here], own_ref[...]) + tn(act_ref[length:, here], other_ref[...])
        part = part.astype(BF16)
        if len(out_refs) == 1:
            out_refs[0][begin : begin + hidden, :] = part
            continue
        keep_x, send_x, keep_y, send_y = out_refs
        half = hidden // 2
        (send_x if offset % 2 else keep_x)[offset // 2, :, :] = part[:half]
        (send_y if offset // 2 else keep_y)[offset % 2, :, :] = part[half:]


def down_grad(act, own, other, chips, position):
    half = act.shape[1]
    width = own.shape[1]
    if square():
        outs = [((2, half // chips // 2, width), BF16)] * 4
    else:
        outs = [((half, width), BF16)]
    return call(
        functools.partial(down_grad_kernel, chips), outs, (act, own, other), position, mib=20
    )


def up_grad_kernel(
    rows, position_ref, own_ref, other_ref, slope_ref, second_ref, second_other_ref, down_ref,
    up_ref, bias_ref, *refs,
):
    out_refs, part_ref = refs[:-1], refs[-1]
    length = own_ref.shape[0]
    total = None
    grads = []
    for which, ref in enumerate((own_ref, other_ref)):
        for at in range(0, length, 2 * ROWS):
            here = slice(which * length + at, which * length + at + 2 * ROWS)
            grad = nt(ref[at : at + 2 * ROWS, :], down_ref[...]) * slope_ref[here, :].astype(F32)
            low = grad.astype(BF16)
            up_ref[here, :] = low
            part = jnp.sum(low.astype(F32), axis=0, keepdims=True)
            total = part if total is None else total + part
    bias_ref[...] = total
    part = tn(second_ref[...], up_ref[:length, :]) + tn(second_other_ref[...], up_ref[length:, :])
    if len(out_refs) == 1:
        out_refs[0][...] = part.astype(BF16)
        return
    part_ref[...] = part
    keep_x, send_x, keep_y, send_y = out_refs
    for offset in range(4):
        begin = pl.multiple_of((position_ref[0] ^ offset) * (2 * rows), SUBLANES)
        upper = part_ref[pl.ds(begin, rows), :].astype(BF16)
        lower = part_ref[pl.ds(begin + rows, rows), :].astype(BF16)
        (send_x if offset % 2 else keep_x)[offset // 2, :, :] = upper
        (send_y if offset // 2 else keep_y)[offset % 2, :, :] = lower


def up_grad(own, other, slope, second, second_other, down_full, rows, position):
    length, width = own.shape
    half = slope.shape[1]
    steps, block, column = column_specs(half, 512)
    whole = whole_spec((length, width))
    if square():
        outs = [((2, rows, half), BF16)] * 4
        specs = [pl.BlockSpec((2, rows, block), lambda i, at: (0, 0, i))] * 4
    else:
        outs = [((width, half), BF16)]
        specs = [column(width)]
    return call(
        functools.partial(up_grad_kernel, rows),
        [((2 * length, half), BF16), ((1, half), F32), *outs],
        (own, other, slope, second, second_other, down_full),
        position,
        grid=(steps,),
        in_specs=[
            whole, whole, column(2 * length), whole, whole,
            pl.BlockSpec((block, width), lambda i, at: (i, 0)),
        ],
        out_specs=[column(2 * length), column(1), *specs],
        scratch=[pltpu.VMEM((width, block), F32)],
        mib=20,
    )


def inward_kernel(grad_ref, up_ref, own_far, other_ref, own_ref, sem):
    length = other_ref.shape[0]
    own_ref[...] = nt(grad_ref[:length, :], up_ref[...])
    copy = pltpu.make_async_copy(own_ref, own_far, sem)
    copy.start()
    other_ref[...] = nt(grad_ref[length:, :], up_ref[...]).astype(BF16)
    copy.wait()


def join_kernel(hidden, position_ref, mine_ref, other_ref, out_ref):
    for at in range(mine_ref.shape[1] // hidden):
        here = slice(hidden * at, hidden * (at + 1))
        for core, ref in enumerate((mine_ref, other_ref)):
            begin = (2 * at + (position_ref[0] + core) % 2) * hidden
            out_ref[:, pl.ds(pl.multiple_of(begin, LANES), hidden)] = ref[:, here].astype(F32)


def branch_kernel(
    got_ref, own_far, middle_far, logits_ref, classes_ref, out_ref, vector_ref,
    grad_ref, branch_ref, attended_ref, sums_ref, own_ref, middle_ref, sems,
):
    width = own_ref.shape[1]
    blocks = range(0, own_ref.shape[0], ROWS)
    copies = []
    for at in blocks:
        here = pl.ds(at, ROWS)
        copies.append(
            [
                pltpu.make_async_copy(far.at[here], ref.at[here], sems.at[at // ROWS, which])
                for which, (far, ref) in enumerate(((own_far, own_ref), (middle_far, middle_ref)))
            ]
        )
        for copy in copies[-1]:
            copy.start()
    gain = vector_ref[FORWARD_GAIN : FORWARD_GAIN + 1, :]
    sums = [jnp.zeros((1, width), F32) for _ in range(3)]
    for at in blocks:
        for copy in copies[at // ROWS]:
            copy.wait()
        here = slice(at, at + ROWS)
        grad = own_ref[here, :] + got_ref[here, :].astype(F32)
        normal, inverse = unit(middle_ref[here, :])
        result = tn(logits_ref[:, here], classes_ref[...])
        middle = result + unit_back(grad, normal, inverse, gain)
        grad_ref[here, :] = middle
        branch = middle.astype(BF16)
        branch_ref[here, :] = branch
        attended_ref[here, :] = nt(branch, out_ref[...]).astype(BF16)
        for which, part in enumerate((grad * normal, grad, branch.astype(F32))):
            sums[which] = sums[which] + jnp.sum(part, axis=0, keepdims=True)
    blank = jnp.zeros((SUBLANES - 3, width), F32)
    sums_ref[...] = jnp.concatenate([*sums, blank], axis=0)


def last_kernel(count, rows, hidden, pieces, position_ref, x_ref, low_ref, *refs):
    grad_refs, refs = refs[: 3 * pieces], refs[3 * pieces :]
    heads_ref, attended_ref, branch_ref, grad_ref, vector_ref, *refs = refs
    sums_ref, loss_ref, up_ref, *refs = refs
    stacks, (input_ref, vectors_ref, full_ref) = refs[:-3], refs[-3:]
    width = x_ref.shape[1]

    def grads(which, here):
        parts = [ref[here, :] for ref in grad_refs[which::3]]
        return jnp.concatenate(parts, axis=1) if pieces > 1 else parts[0]

    for at in range(3):
        part = tn(low_ref[...], grads(at, slice(None)))
        full_ref[:, width * at : width * (at + 1)] = part.astype(BF16)
    full_ref[:, 3 * width :] = tn(attended_ref[...], branch_ref[...]).astype(BF16)
    gain = vector_ref[ATTEND_GAIN : ATTEND_GAIN + 1, :]

    def block(at, sums):
        here = pl.ds(pl.multiple_of(at * ROWS, ROWS), ROWS)
        grad_query, grad_key, grad_value = [grads(which, here) for which in range(3)]
        grad = (
            nt(grad_query, heads_ref[:, :width])
            + nt(grad_key, heads_ref[:, width : 2 * width])
            + nt(grad_value, heads_ref[:, 2 * width :])
        )
        normal, inverse = unit(x_ref[here, :].astype(F32))
        input_ref[here, :] = grad_ref[here, :] + unit_back(grad, normal, inverse, gain)
        parts = (grad * normal, grad, grad_query.astype(F32), grad_value.astype(F32))
        return tuple(
            total + jnp.sum(part, axis=0, keepdims=True) for total, part in zip(sums, parts)
        )

    zero = jnp.zeros((1, width), F32)
    sums = lax.fori_loop(0, x_ref.shape[0] // ROWS, block, (zero,) * 4)
    vectors = jnp.concatenate(
        [*sums, sums_ref[2:3, :], sums_ref[0:1, :], sums_ref[1:2, :], loss_ref[2:3, :]], axis=0
    )
    vectors_ref[...] = vectors
    blank = jnp.zeros((VECTORS - 1, hidden), F32)
    lanes = jnp.concatenate([loss_ref[:2, :LANES], jnp.zeros((VECTORS - 2, LANES), F32)], axis=0)
    for which, stack in enumerate(stacks):

        def slab(step, carry, which=which, stack=stack):
            place_at = position_ref[which * (count // 2) + step]
            begin = pl.multiple_of(place_at * rows, SUBLANES)
            short = pltpu.roll(vectors, width - begin, 1)[:, :LANES]
            if which == 0:
                hidden_at = pl.multiple_of(lax.div(place_at, 2) * hidden, LANES)
                bias = jnp.concatenate([up_ref[:, pl.ds(hidden_at, hidden)], blank], axis=0)
            else:
                bias = jnp.zeros((VECTORS, hidden), F32)
            row = jnp.concatenate([short, bias, lanes], axis=1).astype(BF16)
            pad = jnp.zeros((VECTORS, 4 * width - row.shape[1]), BF16)
            row = jnp.concatenate([row, pad], axis=1)
            picks = (2 * (step % 2) + step // 2, 4 + step)
            for side, pick in enumerate(picks):
                here = slice(2 * width * side, 2 * width * (side + 1))
                stack[pick, :rows, :] = full_ref[pl.ds(begin, rows), here]
                stack[pick, rows:, :] = row[:, here]
            return carry

        lax.fori_loop(0, count // 2, slab, 0)


def settle_kernel(rows, hidden, place_ref, *refs):
    totals, outers, refs = refs[:2], refs[2:4], refs[4:]
    heads_ref, out_ref, short_ref, loss_ref, count_ref = refs
    width = out_ref.shape[1]
    inner = (place_ref[0] == 1) | (place_ref[0] == 2)
    left, right = [
        jnp.where(inner, total[...], outer[...]).astype(F32) for total, outer in zip(totals, outers)
    ]
    heads_ref[:, : 2 * width] = left[:rows]
    heads_ref[:, 2 * width :] = right[:rows, :width]
    out_ref[...] = right[:rows, width:]
    short_ref[...] = left[rows:]
    lanes = left[rows:, LANES + hidden : 2 * LANES + hidden]
    loss_ref[0] = jnp.sum(lanes[0:1])
    count_ref[0] = jnp.sum(lanes[1:2]).astype(jnp.int32)


def swap(values, bit):
    return lax.ppermute(values, "wide", [(i, i ^ bit) for i in range(lax.axis_size("wide"))])


def same_core_groups():
    chips = lax.axis_size("wide") // 2
    return [[2 * chip + core for chip in range(chips)] for core in range(2)]


def square():
    return lax.axis_size("wide") == 8


def spread_chips(shard):
    return lax.all_gather(shard, "wide", axis=0, axis_index_groups=same_core_groups())


def add_low(*parts):
    return sum(part.astype(F32) for part in parts).astype(BF16)


def collect_chips(parts):
    return lax.psum_scatter(
        parts, "wide", scatter_dimension=0, axis_index_groups=same_core_groups()
    )


def after(values, *gates):
    leaves, tree = jax.tree.flatten(values)
    held = lax.optimization_barrier((*leaves, *jax.tree.leaves(gates)))
    return jax.tree.unflatten(tree, held[: len(leaves)])


INWARD, ACROSS, OUTWARD = [(0, 1), (3, 2)], [(1, 2), (2, 1)], [(1, 0), (2, 3)]


def hop(parts, pairs):
    return [lax.ppermute(part, "narrow", pairs) for part in parts]


def add_each(left, right):
    return [add_low(a, b) for a, b in zip(left, right)]


def settle(total, outer):
    place_at = lax.axis_index("narrow")
    return jnp.where((place_at == 1) | (place_at == 2), total, outer)


def sum_narrow(shard):
    if lax.axis_size("narrow") != 4:
        return lax.psum(shard, "narrow")
    half = add_low(shard, *hop([shard], INWARD))
    total = add_low(half, *hop([half], ACROSS))
    return settle(total, *hop([total], OUTWARD))


def local(
    layer_input, segments, targets, loss_mask, readout,
    attend_gain, attend_shift, heads_weight, query_bias, value_bias, output_weight, output_bias,
    forward_gain, forward_shift, up_weight, up_bias, down_weight, down_bias,
):
    length = layer_input.shape[1]
    width = layer_input.shape[2]
    wide = lax.axis_size("wide")
    chips = wide // 2
    core = lax.axis_index("wide") % 2
    chip = lax.axis_index("wide") // 2
    rows = heads_weight.shape[0]
    hidden = up_bias.shape[0]
    half = chips * hidden
    x = layer_input[0]
    classes = readout.T
    vmem = pl.BlockSpec(memory_space=pltpu.VMEM)
    far_away = pl.BlockSpec(memory_space=pltpu.HBM)

    def by_core(mine, other, axis):
        return jnp.where(
            core == 0, jnp.stack([mine, other], axis), jnp.stack([other, mine], axis)
        )

    def mine_of(values, axis, flip=0):
        return lax.dynamic_index_in_dim(values, core ^ flip, axis, keepdims=False)

    short = jnp.stack(
        [
            attend_gain, attend_shift, query_bias, value_bias,
            output_bias, forward_gain, forward_shift, down_bias,
        ]
    )
    core_position = core.reshape(1).astype(jnp.int32)
    chip_position = chip.reshape(1).astype(jnp.int32)
    if square():
        offsets = jnp.arange(4, dtype=jnp.int32)
        (slab,) = call(
            slab_kernel,
            [((rows + VECTORS, 4 * width), BF16)],
            (heads_weight, output_weight, short, up_bias[None]),
        )
        near_x, near_y, far = swap(slab, 2), swap(slab, 4), swap(slab, 6)
        swapped = swap(slab, 1)
        devices = 2 * (chip ^ offsets) + core
        positions = jnp.concatenate([devices, devices ^ 1]).astype(jnp.int32)
        up_weight, positions = after([up_weight, positions], near_x, swapped)
        up_x, up_y = swap(up_weight, 2), swap(up_weight, 4)
        swapped_x = swap(near_x, 1)
        near_y, far = after([near_y, far], swapped_x)
        slabs = [slab, near_x, near_y, far, swapped, swapped_x, swap(near_y, 1), swap(far, 1)]
        first_low, joined, heads_full, output_full, vectors, up_bias_half = call(
            functools.partial(project_kernel, len(slabs), rows, hidden),
            [
                ((length, width), BF16), ((length, 3 * width), BF16), ((width, 3 * width), BF16),
                ((width, width), BF16), ((VECTORS, width), F32), ((VECTORS, half), F32),
            ],
            (x, *slabs),
            positions,
            in_specs=[pl.BlockSpec(memory_space=pltpu.VMEM)]
            + [pl.BlockSpec(memory_space=pltpu.HBM)] * len(slabs),
            scratch=[
                pltpu.VMEM((len(slabs), VECTORS, LANES + hidden), BF16),
                pltpu.SemaphoreType.DMA((len(slabs), 3)),
            ],
            mib=20,
        )
    else:
        tail = jnp.concatenate([short.reshape(1, 8 * rows), up_bias[None]], axis=1)
        tail = jnp.pad(tail, ((0, 0), (0, 4 * width - tail.shape[1])))
        slab = jnp.concatenate(
            [jnp.concatenate([heads_weight, output_weight], axis=1), tail], axis=0
        )
        slabs = lax.all_gather(slab, "wide", axis=0)
        attend_full = slabs[:, :rows].reshape(width, 4 * width)
        heads_full = attend_full[:, : 3 * width]
        output_full = attend_full[:, 3 * width :]
        last = slabs[:, rows].astype(F32)
        vectors = last[:, : 8 * rows].reshape(wide, 8, rows).transpose(1, 0, 2).reshape(8, width)
        up_bias_half = mine_of(last[:, 8 * rows : 8 * rows + hidden].reshape(chips, 2, hidden), 1)
        up_bias_half = jnp.broadcast_to(up_bias_half.reshape(1, half), (VECTORS, half))
        positions = jnp.zeros((1,), jnp.int32)
        first_low, joined = call(
            functools.partial(project_kernel, 0, rows, hidden),
            [((length, width), BF16), ((length, 3 * width), BF16)],
            (x, heads_full, vectors),
            positions,
            mib=20,
        )
        up_view = up_weight.reshape(rows, chips, 2, hidden)
        up_pair = by_core(
            mine_of(up_view, 2).reshape(rows, half),
            swap(mine_of(up_view, 2, 1).reshape(rows, half), 1),
            0,
        ).reshape(2 * rows, half)
        up_parts = [spread_chips(up_pair).reshape(width, half)]
        down_parts = [spread_chips(down_weight).reshape(half, width)]
        up_positions = down_positions = positions

    attended, across, lse = attend(joined, segments)
    if square():
        up_x, up_y = after([up_x, up_y], attended)
        cut = rows // 2
        passed = [up_y[:cut], up_x[cut:]]
        (attended,) = after([attended], passed)
        near = [up_weight, up_x, up_y]
        near_swapped = [swap(part, 1) for part in near]
        passed = [swap(passed[0], 2), swap(passed[1], 4)]
        up_parts = [*near, *passed, *near_swapped, *[swap(part, 1) for part in passed]]
        at = jnp.arange(11, dtype=jnp.int32)
        part = at % 5
        device = 2 * (chip ^ jnp.minimum(part, 3)) + (core ^ (at // 5))
        up_positions = jnp.where(part < 3, device, 2 * device + part - 3)
        up_positions = jnp.where(at < 10, up_positions, core).astype(jnp.int32)
        middle_row = hidden // 2
        upper, lower = after(
            [down_weight[:middle_row], down_weight[middle_row:]], up_x, up_y
        )
        lower_x, upper_y = swap(lower, 2), swap(upper, 4)
        upper_x, lower_y = swap(upper, 2), swap(lower, 4)
        down_parts = [
            down_weight, upper_x, lower_x, upper_y, lower_y
        ]
        at = jnp.arange(7, dtype=jnp.int32)
        down_positions = jnp.where(at == 0, chip, 2 * (chip ^ ((at + 1) // 2)) + (at + 1) % 2)
    middle, second_low = call(
        middle_kernel,
        [((length, width), F32), ((length, width), BF16)],
        (x, attended, output_full, vectors),
    )

    if square():
        (second_other,) = after([second_low], near_swapped)
        second_other = swap(second_other, 1)
    else:
        second_other = swap(second_low, 1)
    activated, slope, up_full = up_project(
        second_low, second_other, up_bias_half, up_parts, up_positions, hidden
    )
    if square():
        passed_x, passed_y = after([upper_y, lower_x], activated)
        far = [swap(passed_x, 2), swap(passed_y, 4)]
        outward, outward_other, down_full = down_project_square(
            activated, down_parts, lambda total: after(far, total), down_positions
        )
    else:
        outward, outward_other, down_full = down_project(activated, down_parts, down_positions)
    result_low, grad_down, grad_logits, loss_sums = call(
        loss_kernel,
        [
            ((length, width), BF16), ((length, width), BF16), (classes.shape[:1] + (length,), BF16),
            ((SUBLANES, width), F32),
        ],
        (middle, outward, swap(outward_other, 1), vectors, classes, targets, loss_mask),
    )

    grad_down_other = swap(grad_down, 1)
    down_parts = down_grad(activated, grad_down, grad_down_other, chips, chip_position)
    if square():
        keep_dx, send_dx, keep_dy, send_dy = down_parts
        down_first = [swap(send_dx, 2), swap(send_dy, 4)]
        (grad_down_other,) = after([grad_down_other], send_dx)
    grad_up, up_bias_part, *up_parts = up_grad(
        grad_down, grad_down_other, slope, second_low, second_other, down_full, rows, chip_position
    )
    inward, inward_other = call(
        inward_kernel,
        [((length, width), F32), ((length, width), BF16)],
        (grad_up, up_full),
        out_specs=[far_away, vmem],
        scratch=[pltpu.VMEM((length, width), F32), pltpu.SemaphoreType.DMA],
        mib=20,
    )
    got_inward = swap(inward_other, 1)
    if square():
        down_second = [
            add_low(keep_dx[1], down_first[0][1]), add_low(keep_dy[1], down_first[1][1])
        ]
        (got_inward,) = after([got_inward], down_second)
        keep_ux, send_ux, keep_uy, send_uy = up_parts
        send_ux, send_uy = after([send_ux, send_uy], down_second)
        down_got = [swap(down_second[0], 4), swap(down_second[1], 2)]
        up_first = [swap(send_ux, 2), swap(send_uy, 4)]
    grad_middle, grad_branch, grad_attended, branch_sums = call(
        branch_kernel,
        [
            ((length, width), F32), ((length, width), BF16), ((length, width), BF16),
            ((SUBLANES, width), F32),
        ],
        (got_inward, inward, middle, grad_logits, classes, output_full, vectors),
        in_specs=[vmem, far_away, far_away, vmem, vmem, vmem, vmem],
        scratch=[
            *[pltpu.VMEM((length, width), F32)] * 2,
            pltpu.SemaphoreType.DMA((length // ROWS, 2)),
        ],
        mib=24,
    )

    if square():
        attend_grads = attend_back(joined, segments, grad_attended, across, lse)
        down_got = after(down_got, attend_grads[0])
        down_narrow = [
            add_low(keep_dx[0], down_first[0][0], down_got[0]),
            add_low(keep_dy[0], down_first[1][0], down_got[1]),
        ]
        down_in = hop(down_narrow, INWARD)
        attend_grads = after(attend_grads, down_narrow)
    else:
        attend_grads = attend_back(joined, segments, grad_attended, across, lse)
    stack_shape = ((8, rows + VECTORS, 2 * width), BF16)
    *stacks, input_grad, short_sums, attend_part = call(
        functools.partial(last_kernel, 8 if square() else 0, rows, hidden, len(attend_grads) // 3),
        ([stack_shape] * 2 if square() else [])
        + [((length, width), F32), ((VECTORS, width), F32), ((width, 4 * width), BF16)],
        (
            x, first_low, *attend_grads, heads_full, attended, grad_branch,
            grad_middle, vectors, branch_sums, loss_sums, up_bias_part,
        ),
        positions,
        mib=40,
    )
    if square():
        mine, others = stacks
        mine_got = swap(others, 1)
        up_first = after(up_first, mine)
        up_second = [add_low(keep_ux[1], up_first[0][1]), add_low(keep_uy[1], up_first[1][1])]
        up_got = [swap(up_second[0], 4), swap(up_second[1], 2)]

        down_in = after(down_in, up_second)
        down_half = jnp.concatenate(add_each(down_narrow, down_in))
        (down_mid,) = hop([down_half], ACROSS)

        (mine_got,) = after([mine_got], down_half)
        both = add_low(mine, mine_got)
        side_first = [swap(both[2:4], 2), swap(both[6:8], 4)]

        up_got = after(up_got, both)
        up_narrow = [
            add_low(keep_ux[0], up_first[0][0], up_got[0]),
            add_low(keep_uy[0], up_first[1][0], up_got[1]),
        ]
        up_in = hop(up_narrow, INWARD)

        side_first = after(side_first, up_narrow)
        side_second = [add_low(both[1], side_first[0][1]), add_low(both[5], side_first[1][1])]
        side_got = [swap(side_second[0], 4), swap(side_second[1], 2)]

        (down_mid,) = after([down_mid], side_second)
        down_total = add_low(down_half, down_mid)
        (down_out,) = hop([down_total], OUTWARD)

        side_got = after(side_got, down_total)
        slab_narrow = [
            add_low(both[0], side_first[0][0], side_got[0]),
            add_low(both[4], side_first[1][0], side_got[1]),
        ]
        slab_in = hop(slab_narrow, INWARD)

        (came,) = after(up_in[:1], slab_narrow)
        up_half = [add_low(up_narrow[0], came)]
        up_mid = hop(up_half, ACROSS)

        (came,) = after(up_in[1:], up_half)
        up_half.append(add_low(up_narrow[1], came))
        up_mid += hop(up_half[1:], ACROSS)

        (came,) = after(up_mid[:1], up_half[1])
        up_total = [add_low(up_half[0], came)]
        up_out = hop(up_total, OUTWARD)

        (came,) = after(slab_in[:1], up_total)
        slab_half = [add_low(slab_narrow[0], came)]
        slab_mid = hop(slab_half, ACROSS)

        (came,) = after(up_mid[1:], slab_half)
        up_total.append(add_low(up_half[1], came))
        up_out += hop(up_total[1:], OUTWARD)

        (came,) = after(slab_in[1:], up_total[1])
        slab_half.append(add_low(slab_narrow[1], came))
        slab_mid += hop(slab_half[1:], ACROSS)

        gate = slab_half[1]
        slab_total, slab_out = [], []
        for at in range(2):
            (came,) = after([slab_mid[at]], gate)
            slab_total.append(add_low(slab_half[at], came))
            slab_out += hop(slab_total[-1:], OUTWARD)
            gate = slab_total[-1:]

        (down_out,) = after([down_out], gate)
        down_weight_sum = settle(down_total, down_out).astype(F32)
        up_out = after(up_out, down_weight_sum, slab_out[0])
        upper, lower = [settle(*pair) for pair in zip(up_total, up_out)]
        first = core == 0
        (up_weight_sum,) = call(
            functools.partial(join_kernel, hidden),
            [((rows, 2 * half), F32)],
            (jnp.where(first, upper, lower), swap(jnp.where(first, lower, upper), 1)),
            core_position,
        )
        slab_out = after(slab_out, upper, lower)
        scalar = pl.BlockSpec(memory_space=pltpu.SMEM)
        heads_sum, output_sum, short, loss_sum, token_count = call(
            functools.partial(settle_kernel, rows, hidden),
            [
                ((rows, 3 * width), F32), ((rows, width), F32), ((VECTORS, 2 * width), F32),
                ((1,), F32), ((1,), jnp.int32),
            ],
            (*slab_total, *slab_out),
            lax.axis_index("narrow").reshape(1).astype(jnp.int32),
            out_specs=[vmem, vmem, vmem, scalar, scalar],
        )
        vectors_sum = short[:, :rows]
        up_bias_grad = short[0, LANES : LANES + hidden]
        loss_sum, token_count = loss_sum.reshape(()), token_count.reshape(())
    else:
        down_weight_sum = collect_chips(down_parts[0].reshape(chips, hidden, width))
        down_weight_sum = sum_narrow(down_weight_sum).astype(F32)
        up_sum = sum_narrow(collect_chips(up_parts[0].reshape(chips, 2 * rows, half)))
        up_sum = up_sum.reshape(2, rows, chips, hidden)
        up_weight_sum = by_core(mine_of(up_sum, 0), swap(mine_of(up_sum, 0, 1), 1), 2)
        up_weight_sum = up_weight_sum.reshape(rows, 2 * half).astype(F32)
        short = short_sums.reshape(8, wide, rows).transpose(1, 0, 2).reshape(wide, 8 * rows)
        up_bias_rows = up_bias_part.reshape(chips, hidden)
        up_bias_rows = by_core(up_bias_rows, jnp.zeros_like(up_bias_rows), 1).reshape(wide, hidden)
        shared = jnp.broadcast_to(loss_sums[:1, :LANES], (wide, LANES))
        row = jnp.concatenate([short, up_bias_rows, shared], axis=1).astype(BF16)
        row = jnp.pad(row, ((0, 0), (0, 4 * width - row.shape[1])))
        slab = jnp.concatenate([attend_part.reshape(wide, rows, 4 * width), row[:, None]], axis=1)
        slab = sum_narrow(lax.psum_scatter(slab, "wide", scatter_dimension=0)).astype(F32)
        vectors_sum = slab[rows, : 8 * rows].reshape(8, rows)
        heads_sum, output_sum = slab[:rows, : 3 * width], slab[:rows, 3 * width :]
        up_bias_grad = slab[rows, 8 * rows : 8 * rows + hidden]
        loss_sum = jnp.sum(slab[rows, 8 * rows + hidden : 8 * rows + hidden + LANES])
        token_count = lax.psum(jnp.sum(loss_mask), ("narrow", "wide"))
    return (
        result_low[None],
        input_grad[None],
        vectors_sum[ATTEND_GAIN],
        vectors_sum[ATTEND_SHIFT],
        heads_sum,
        vectors_sum[QUERY_BIAS],
        vectors_sum[VALUE_BIAS],
        output_sum,
        vectors_sum[OUTPUT_BIAS],
        vectors_sum[FORWARD_GAIN],
        vectors_sum[FORWARD_SHIFT],
        up_weight_sum,
        up_bias_grad,
        down_weight_sum,
        vectors_sum[DOWN_BIAS],
        loss_sum,
        token_count,
    )


def solution(mesh):
    in_specs = (
        P(("narrow", "wide"), None, None),
        P(("narrow", "wide"), None),
        P(("narrow", "wide"), None),
        P(("narrow", "wide"), None),
        P(),
        P("wide"),
        P("wide"),
        P("wide", None),
        P("wide"),
        P("wide"),
        P("wide", None),
        P("wide"),
        P("wide"),
        P("wide"),
        P("wide", None),
        P("wide"),
        P("wide", None),
        P("wide"),
    )
    out_specs = (
        P(("narrow", "wide"), None, None),
        P(("narrow", "wide"), None, None),
        P("wide"),
        P("wide"),
        P("wide", None),
        P("wide"),
        P("wide"),
        P("wide", None),
        P("wide"),
        P("wide"),
        P("wide"),
        P("wide", None),
        P("wide"),
        P("wide", None),
        P("wide"),
        P(),
        P(),
    )
    return jax.shard_map(local, mesh=mesh, in_specs=in_specs, out_specs=out_specs, check_vma=False)
```

profile of v0, /device:TPU:0, one launch (start us, length us, event | category | flops | bytes accessed | tf_op | source)
XLA Modules:
  0.0 241.6 jit_solution(13767807478223809278)
XLA Ops:
  4.1 3.0 %collective-permute-start = (bf16[88,2560]{1,0:T(8,128)(2,1)S(1)}, bf16[88,2560]{1,0:T(8,128)(2,1)S(1)}, u32[]{:S(2)}, u32[]{:S(2)}) collective-permute-start(bf16[88,2560]{1,0:T(8,128)(2,1)S(1)} %shard_map.305.refs_0_), channel_id=1, source_target_pairs={{0,2},{1,3},{2,0},{3,1},{4,6},{5,7},{6,4},{7,5},{8,10},{9,11},{10,... | collective-permute-start | bytes 1351688 | tf_op jit(solution)/shard_map/ppermute | solution.py:774
  8.7 9.6 %collective-permute-done.refs_1_ = bf16[88,2560]{1,0:T(8,128)(2,1)S(1)} collective-permute-done((bf16[88,2560]{1,0:T(8,128)(2,1)S(1)}, bf16[88,2560]{1,0:T(8,128)(2,1)S(1)}, u32[]{:S(2)}, u32[]{:S(2)}) %collective-permute-start) | collective-permute-done | bytes 450592 | tf_op jit(solution)/shard_map/ppermute | solution.py:774
  18.4 2.1 collective-permute-start.7
  22.0 8.0 %collective-permute-done.2.refs_2_ = bf16[88,2560]{1,0:T(8,128)(2,1)S(1)} collective-permute-done((bf16[88,2560]{1,0:T(8,128)(2,1)S(1)}, bf16[88,2560]{1,0:T(8,128)(2,1)S(1)}, u32[]{:S(2)}, u32[]{:S(2)}) %collective-permute-start.2) | collective-permute-done | bytes 450592 | tf_op jit(solution)/shard_map/ppermute | solution.py:774
  34.4 5.0 %shard_map.306 = (bf16[512,640]{1,0:T(8,128)(2,1)S(1)}, bf16[512,1920]{1,0:T(8,128)(2,1)S(1)}, bf16[640,1920]{1,0:T(8,128)(2,1)S(1)}, bf16[640,640]{1,0:T(8,128)...) custom-call(s32[8]{0:T(128)S(1)} %pad_add_fusion.position_ref, bf16[512,640]{1,0:T(8,128)(2,1)S(1)} %bitcast.69, ...), custom_call_target="tpu_custom_call" | custom-call | flops 1 | bytes 1 | tf_op jit(solution)/shard_map/pallas_call | solution.py:56
  39.4 7.9 %shard_map.307 = (bf16[512,640]{1,0:T(8,128)(2,1)S(1)}, f32[640,512]{1,0:T(8,128)S(1)}, f32[40,512]{1,0:T(8,128)S(1)}) custom-call(s32[1,512]{1,0:T(1,128)S(1)} %copy-done.31, bf16[512,1920]{1,0:T(8,128)(2,1)S(1)} %get-tuple-element.118.q_ref.k_ref.v_ref, bf16[512,1920]{1,0:T(8,128)(2,1)S(1)} %get-tuple-element.118.q_ref.k_ref.v_ref, ...), custom_call_target="tpu_custom_call" | custom-call | flops 1 | bytes 1 | tf_op jit(solution)/shard_map/pallas_call | solution.py:56
  51.6 8.0 %collective-permute-done.13.refs_3_ = bf16[40,5120]{1,0:T(8,128)(2,1)S(1)} collective-permute-done((bf16[40,5120]{1,0:T(8,128)(2,1)S(1)}, bf16[40,5120]{1,0:T(8,128)(2,1)S(1)}, u32[]{:S(2)}, u32[]{:S(2)}) %collective-permute-start.13) | collective-permute-done | bytes 409632 | tf_op jit(solution)/shard_map/ppermute | solution.py:774
  64.5 9.5 %shard_map.309 = (bf16[1024,2560]{1,0:T(8,128)(2,1)S(1)}, bf16[1024,2560]{1,0:T(8,128)(2,1)S(1)}, bf16[640,2560]{1,0:T(8,128)(2,1)S(1)}) custom-call(s32[11]{0:T(128)S(1)} %compare_select_fusion.1.position_ref, bf16[512,640]{1,0:T(8,128)(2,1)S(1)} %get-tuple-element.128.own_ref.second_ref, ...), custom_call_target="tpu_custom_call" | custom-call | flops 1 | bytes 1 | tf_op jit(solution)/shard_map/pallas_call | solution.py:56
  76.7 4.8 %collective-permute-done.17.refs_1_ = bf16[320,640]{1,0:T(8,128)(2,1)S(1)} collective-permute-done((bf16[320,640]{1,0:T(8,128)(2,1)S(1)}, bf16[320,640]{1,0:T(8,128)(2,1)S(1)}, u32[]{:S(2)}, u32[]{:S(2)}) %collective-permute-start.17) | collective-permute-done | bytes 409632 | tf_op jit(solution)/shard_map/ppermute | solution.py:774
  82.5 4.4 %shard_map.310 = (f32[1024,640]{1,0:T(8,128)S(1)}, bf16[2560,640]{1,0:T(8,128)(2,1)S(1)}) custom-call(s32[7]{0:T(128)S(1)} %compare_select_fusion.2.position_ref, bf16[1024,2560]{1,0:T(8,128)(2,1)S(1)} %get-tuple-element.130.act_ref, bf16[640,640]{1,0:T(8,128)(2,1)S(1)} %copy-done.5, bf16[320,640]{1,0:T(8,128)(2,1)S(1)} %collective-permute-done.17.refs_1_, ...), custom_call_target="tpu_custom_call" | custom-call | flops 1 | bytes 1 | tf_op jit(solution)/shard_map/pallas_call | solution.py:56
  86.9 2.9 %collective-permute-done.21.upper_ref = bf16[320,640]{1,0:T(8,128)(2,1)S(1)} collective-permute-done((bf16[320,640]{1,0:T(8,128)(2,1)S(1)}, bf16[320,640]{1,0:T(8,128)(2,1)S(1)}, u32[]{:S(2)}, u32[]{:S(2)}) %collective-permute-start.21) | collective-permute-done | bytes 409632 | tf_op jit(solution)/shard_map/ppermute | solution.py:774
  90.6 1.9 shard_map.311
  92.6 2.1 collective-permute-done.23.got_ref
  95.9 2.0 collective-permute-done.24.other_ref
  97.9 4.3 %shard_map.313 = (bf16[2,320,640]{2,1,0:T(8,128)(2,1)S(1)}, bf16[2,320,640]{2,1,0:T(8,128)(2,1)S(1)}, bf16[2,320,640]{2,1,0:T(8,128)(2,1)S(1)}, bf16[2,320,640]{2,1,0:T(8,128)(2,1)S(1)}) custom-call(s32[1]{0:T(128)} %bitcast.11.position_ref, bf16[1024,2560]{1,0:T(8,128)(2,1)S(1)} %get-tuple-element.130.act_ref, ...), custom_call_target="tpu_custom_call" | custom-call | flops 1 | bytes 1 | tf_op jit(solution)/shard_map/pallas_call | solution.py:56
  104.3 10.8 %shard_map.314 = (bf16[1024,2560]{1,0:T(8,128)(2,1)S(1)}, f32[1,2560]{1,0:T(1,128)S(1)}, bf16[2,80,2560]{2,1,0:T(8,128)(2,1)S(1)}, bf16[2,80,2560]{2,1,0:T(8,128...) custom-call(s32[1]{0:T(128)} %bitcast.11.position_ref, ...), custom_call_target="tpu_custom_call" | custom-call | flops 1 | bytes 1 | tf_op jit(solution)/shard_map/pallas_call | solution.py:56
  115.2 6.0 %shard_map.315 = (f32[512,640]{1,0:T(8,128)}, bf16[512,640]{1,0:T(8,128)(2,1)}) custom-call(bf16[1024,2560]{1,0:T(8,128)(2,1)S(1)} %get-tuple-element.148.grad_ref, bf16[640,2560]{1,0:T(8,128)(2,1)S(1)} %get-tuple-element.149.up_ref), custom_call_target="tpu_custom_call" | custom-call | flops 1 | bytes 1 | tf_op jit(solution)/shard_map/pallas_call | solution.py:56
  128.7 4.1 %shard_map.316 = (f32[512,640]{1,0:T(8,128)S(1)}, bf16[512,640]{1,0:T(8,128)(2,1)S(1)}, bf16[512,640]{1,0:T(8,128)(2,1)S(1)}, f32[8,640]{1,0:T(8,128)S(1)}) custom-call(bf16[512,640]{1,0:T(8,128)(2,1)S(1)} %collective-permute-done.25.got_ref, f32[512,640]{1,0:T(8,128)} %get-tuple-element.155.own_far, f32[512,640]{1,0:T(8,128)} %copy-done.2, ...), custom_call_target="tpu_custom_call" | custom-call | flops 1 | bytes 1 | tf_op jit(solution)/shard_map/pallas_call | solution.py:56
  132.9 13.0 %shard_map.317 = (bf16[512,640]{1,0:T(8,128)(2,1)S(1)}, bf16[512,640]{1,0:T(8,128)(2,1)S(1)}, bf16[512,640]{1,0:T(8,128)(2,1)S(1)}) custom-call(s32[1,512]{1,0:T(1,128)S(1)} %copy-done.32, bf16[512,1920]{1,0:T(8,128)(2,1)S(1)} %get-tuple-element.118.q_ref.k_ref.v_ref, bf16[512,1920]{1,0:T(8,128)(2,1)S(1)} %get-tuple-element.118.q_ref.k_ref.v_ref, ...), custom_call_target="tpu_custom_call" | custom-call | flops 1 | bytes 1 | tf_op jit(solution)/shard_map/pallas_call | solution.py:56
  147.2 3.5 %collective-permute-start.31 = (bf16[320,640]{1,0:T(8,128)(2,1)S(1)}, bf16[320,640]{1,0:T(8,128)(2,1)S(1)}, u32[]{:S(2)}, u32[]{:S(2)}) collective-permute-start(bf16[320,640]{1,0:T(8,128)(2,1)S(1)} %fusion.3), channel_id=1, source_target_pairs={{0,8},{24,16},{1,9},{25,17},{2,10},{26,18},{3,11},{27,19},{4,12},{... | collective-permute-start | bytes 1228808 | tf_op jit(solution)/shard_map/ppermute | solution.py:810
  153.3 9.7 %shard_map.318 = (bf16[8,88,1280]{2,1,0:T(8,128)(2,1)S(1)}, bf16[8,88,1280]{2,1,0:T(8,128)(2,1)S(1)}, f32[512,640]{1,0:T(8,128)}, f32[8,640]{1,0:T(8,128)}, bf16[640,2560]{1,0:T(8,128)(2,1)}) custom-call(s32[8]{0:T(128)S(1)} %copy-done.36, bf16[512,640]{1,0:T(8,128)(2,1)S(1)} %bitcast.71, bf16[512,640]{1,0:T(8,128)(2,1)S(1)} %copy-done.23, ...), custom_call_target="tpu_custom_call" | custom-call | flops 1 | bytes 1 | tf_op jit(solution)/shard_map/pallas_call | solution.py:56
  164.2 1.6 collective-permute-start.37
  171.4 5.2 %collective-permute-done.37 = bf16[80,2560]{1,0:T(8,128)(2,1)S(1)} collective-permute-done((bf16[80,2560]{1,0:T(8,128)(2,1)S(1)}, bf16[80,2560]{1,0:T(8,128)(2,1)S(1)}, u32[]{:S(2)}, u32[]{:S(2)}) %collective-permute-start.37) | collective-permute-done | bytes 409632 | tf_op jit(solution)/shard_map/ppermute | solution.py:774
  176.6 2.7 %collective-permute-done.38 = bf16[80,2560]{1,0:T(8,128)(2,1)S(1)} collective-permute-done((bf16[80,2560]{1,0:T(8,128)(2,1)S(1)}, bf16[80,2560]{1,0:T(8,128)(2,1)S(1)}, u32[]{:S(2)}, u32[]{:S(2)}) %collective-permute-start.38) | collective-permute-done | bytes 409632 | tf_op jit(solution)/shard_map/ppermute | solution.py:774
  184.2 4.0 %collective-permute-done.35 = bf16[2,88,1280]{2,1,0:T(8,128)(2,1)S(1)} collective-permute-done((bf16[2,88,1280]{2,1,0:T(8,128)(2,1)S(1)}, bf16[2,88,1280]{2,1,0:T(8,128)(2,1)S(1)}, u32[]{:S(2)}, u32[]{:S(2)}) %collective-permute-start.35) | collective-permute-done | bytes 450592 | tf_op jit(solution)/shard_map/ppermute | solution.py:774
  191.4 3.8 %collective-permute-done.39 = bf16[88,1280]{1,0:T(8,128)(2,1)S(1)} collective-permute-done((bf16[88,1280]{1,0:T(8,128)(2,1)S(1)}, bf16[88,1280]{1,0:T(8,128)(2,1)S(1)}, u32[]{:S(2)}, u32[]{:S(2)}) %collective-permute-start.39) | collective-permute-done | bytes 225312 | tf_op jit(solution)/shard_map/ppermute | solution.py:774
  199.0 2.5 %collective-permute-done.45 = bf16[80,2560]{1,0:T(8,128)(2,1)S(1)} collective-permute-done((bf16[80,2560]{1,0:T(8,128)(2,1)S(1)}, bf16[80,2560]{1,0:T(8,128)(2,1)S(1)}, u32[]{:S(2)}, u32[]{:S(2)}) %collective-permute-start.45) | collective-permute-done | bytes 409632 | tf_op jit(solution)/shard_map/ppermute | solution.py:810
  203.7 2.6 %collective-permute-done.42 = bf16[88,1280]{1,0:T(8,128)(2,1)S(1)} collective-permute-done((bf16[88,1280]{1,0:T(8,128)(2,1)S(1)}, bf16[88,1280]{1,0:T(8,128)(2,1)S(1)}, u32[]{:S(2)}, u32[]{:S(2)}) %collective-permute-start.42) | collective-permute-done | bytes 225312 | tf_op jit(solution)/shard_map/ppermute | solution.py:810
  214.3 7.5 %collective-permute-done.52 = bf16[80,2560]{1,0:T(8,128)(2,1)S(1)} collective-permute-done((bf16[80,2560]{1,0:T(8,128)(2,1)S(1)}, bf16[80,2560]{1,0:T(8,128)(2,1)S(1)}, u32[]{:S(2)}, u32[]{:S(2)}) %collective-permute-start.52) | collective-permute-done | bytes 409632 | tf_op jit(solution)/shard_map/ppermute | solution.py:810
  221.8 10.2 %collective-permute-done.53 = bf16[80,2560]{1,0:T(8,128)(2,1)S(1)} collective-permute-done((bf16[80,2560]{1,0:T(8,128)(2,1)S(1)}, bf16[80,2560]{1,0:T(8,128)(2,1)S(1)}, u32[]{:S(2)}, u32[]{:S(2)}) %collective-permute-start.53) | collective-permute-done | bytes 409632 | tf_op jit(solution)/shard_map/ppermute | solution.py:810
  232.0 3.7 %collective-permute-done.50.refs_2_ = bf16[88,1280]{1,0:T(8,128)(2,1)S(1)} collective-permute-done((bf16[88,1280]{1,0:T(8,128)(2,1)S(1)}, bf16[88,1280]{1,0:T(8,128)(2,1)S(1)}, u32[]{:S(2)}, u32[]{:S(2)}) %collective-permute-start.50) | collective-permute-done | bytes 225312 | tf_op jit(solution)/shard_map/ppermute | solution.py:810
  236.0 2.2 collective-permute-done.51.refs_3_
  (229 shorter events, 71.5 us)
Async XLA Ops:
  4.1 14.2 %collective-permute-start = (bf16[88,2560]{1,0:T(8,128)(2,1)S(1)}, bf16[88,2560]{1,0:T(8,128)(2,1)S(1)}, u32[]{:S(2)}, u32[]{:S(2)}) collective-permute-start(bf16[88,2560]{1,0:T(8,128)(2,1)S(1)} %shard_map.305.refs_0_), channel_id=1, source_target_pairs={{0,2},{1,3},{2,0},{3,1},{4,6},{5,7},{6,4},{7,5},{8,10},{9,11},{10,... | collective-permute-start | bytes 1351688 | tf_op jit(solution)/shard_map/ppermute | solution.py:774
  7.1 22.9 %collective-permute-start.2 = (bf16[88,2560]{1,0:T(8,128)(2,1)S(1)}, bf16[88,2560]{1,0:T(8,128)(2,1)S(1)}, u32[]{:S(2)}, u32[]{:S(2)}) collective-permute-start(bf16[88,2560]{1,0:T(8,128)(2,1)S(1)} %shard_map.305.refs_0_), channel_id=1, source_target_pairs={{0,4},{1,5},{2,6},{3,7},{4,0},{5,1},{6,2},{7,3},{8,12},{9,13},{10,... | collective-permute-start | bytes 1351688 | tf_op jit(solution)/shard_map/ppermute | solution.py:774
  8.6 21.4 %collective-permute-start.3 = (bf16[88,2560]{1,0:T(8,128)(2,1)S(1)}, bf16[88,2560]{1,0:T(8,128)(2,1)S(1)}, u32[]{:S(2)}, u32[]{:S(2)}) collective-permute-start(bf16[88,2560]{1,0:T(8,128)(2,1)S(1)} %shard_map.305.refs_0_), channel_id=1, source_target_pairs={{0,6},{1,7},{2,4},{3,5},{4,2},{5,3},{6,0},{7,1},{8,14},{9,15},{10,... | collective-permute-start | bytes 1351688 | tf_op jit(solution)/shard_map/ppermute | solution.py:774
  18.4 29.0 %collective-permute-start.7 = (bf16[80,5120]{1,0:T(8,128)(2,1)}, bf16[80,5120]{1,0:T(8,128)(2,1)S(1)}, u32[]{:S(2)}, u32[]{:S(2)}) collective-permute-start(bf16[80,5120]{1,0:T(8,128)(2,1)} %refs_0_.1), channel_id=1, source_target_pairs={{0,2},{1,3},{2,0},{3,1},{4,6},{5,7},{6,4},{7,5},{8,10},{9,11},{10,... | collective-permute-start | bytes 2457608 | tf_op jit(solution)/shard_map/ppermute | solution.py:774
  20.4 26.9 %collective-permute-start.8 = (bf16[80,5120]{1,0:T(8,128)(2,1)}, bf16[80,5120]{1,0:T(8,128)(2,1)S(1)}, u32[]{:S(2)}, u32[]{:S(2)}) collective-permute-start(bf16[80,5120]{1,0:T(8,128)(2,1)} %refs_0_.1), channel_id=1, source_target_pairs={{0,4},{1,5},{2,6},{3,7},{4,0},{5,1},{6,2},{7,3},{8,12},{9,13},{10,... | collective-permute-start | bytes 2457608 | tf_op jit(solution)/shard_map/ppermute | solution.py:774
  30.6 20.8 %collective-permute-start.9 = (bf16[80,5120]{1,0:T(8,128)(2,1)}, bf16[80,5120]{1,0:T(8,128)(2,1)S(1)}, u32[]{:S(2)}, u32[]{:S(2)}) collective-permute-start(bf16[80,5120]{1,0:T(8,128)(2,1)} %refs_0_.1), channel_id=1, source_target_pairs={{0,1},{1,0},{2,3},{3,2},{4,5},{5,4},{6,7},{7,6},{8,9},{9,8},{10,11... | collective-permute-start | bytes 2457608 | tf_op jit(solution)/shard_map/ppermute | solution.py:774
  51.4 13.1 %collective-permute-start.12 = (bf16[512,640]{1,0:T(8,128)(2,1)S(1)}, bf16[512,640]{1,0:T(8,128)(2,1)S(1)}, u32[]{:S(2)}, u32[]{:S(2)}) collective-permute-start(bf16[512,640]{1,0:T(8,128)(2,1)S(1)} %get-tuple-element.128.own_ref.second_ref), channel_id=1, source_target_pairs={{0,1},{1,0},{2,3},{3,2},{4,5},{5,4},{6,7},{7,6},{8,9},{9,8},{10,11... | collective-permute-start | bytes 1966088 | tf_op jit(solution)/shard_map/ppermute | solution.py:774
  60.4 13.7 %collective-permute-start.18 = (bf16[320,640]{1,0:T(8,128)(2,1)S(1)}, bf16[320,640]{1,0:T(8,128)(2,1)S(1)}, u32[]{:S(2)}, u32[]{:S(2)}) collective-permute-start(bf16[320,640]{1,0:T(8,128)(2,1)S(1)} %get-tuple-element.132), channel_id=1, source_target_pairs={{0,2},{1,3},{2,0},{3,1},{4,6},{5,7},{6,4},{7,5},{8,10},{9,11},{10,... | collective-permute-start | bytes 1228808 | tf_op jit(solution)/shard_map/ppermute | solution.py:774
  61.4 12.6 %collective-permute-start.19 = (bf16[320,640]{1,0:T(8,128)(2,1)S(1)}, bf16[320,640]{1,0:T(8,128)(2,1)S(1)}, u32[]{:S(2)}, u32[]{:S(2)}) collective-permute-start(bf16[320,640]{1,0:T(8,128)(2,1)S(1)} %get-tuple-element.131), channel_id=1, source_target_pairs={{0,4},{1,5},{2,6},{3,7},{4,0},{5,1},{6,2},{7,3},{8,12},{9,13},{10,... | collective-permute-start | bytes 1228808 | tf_op jit(solution)/shard_map/ppermute | solution.py:774
  63.0 18.5 %collective-permute-start.17 = (bf16[320,640]{1,0:T(8,128)(2,1)S(1)}, bf16[320,640]{1,0:T(8,128)(2,1)S(1)}, u32[]{:S(2)}, u32[]{:S(2)}) collective-permute-start(bf16[320,640]{1,0:T(8,128)(2,1)S(1)} %get-tuple-element.131), channel_id=1, source_target_pairs={{0,2},{1,3},{2,0},{3,1},{4,6},{5,7},{6,4},{7,5},{8,10},{9,11},{10,... | collective-permute-start | bytes 1228808 | tf_op jit(solution)/shard_map/ppermute | solution.py:774
  63.7 18.8 %collective-permute-start.20 = (bf16[320,640]{1,0:T(8,128)(2,1)S(1)}, bf16[320,640]{1,0:T(8,128)(2,1)S(1)}, u32[]{:S(2)}, u32[]{:S(2)}) collective-permute-start(bf16[320,640]{1,0:T(8,128)(2,1)S(1)} %get-tuple-element.132), channel_id=1, source_target_pairs={{0,4},{1,5},{2,6},{3,7},{4,0},{5,1},{6,2},{7,3},{8,12},{9,13},{10,... | collective-permute-start | bytes 1228808 | tf_op jit(solution)/shard_map/ppermute | solution.py:774
  74.1 15.7 %collective-permute-start.21 = (bf16[320,640]{1,0:T(8,128)(2,1)S(1)}, bf16[320,640]{1,0:T(8,128)(2,1)S(1)}, u32[]{:S(2)}, u32[]{:S(2)}) collective-permute-start(bf16[320,640]{1,0:T(8,128)(2,1)S(1)} %collective-permute-done.19.refs_3_), channel_id=1, source_target_pairs={{0,2},{1,3},{2,0},{3,1},{4,6},{5,7},{6,4},{7,5},{8,10},{9,11},{10,... | collective-permute-start | bytes 1228808 | tf_op jit(solution)/shard_map/ppermute | solution.py:774
  75.2 15.4 %collective-permute-start.22 = (bf16[320,640]{1,0:T(8,128)(2,1)S(1)}, bf16[320,640]{1,0:T(8,128)(2,1)S(1)}, u32[]{:S(2)}, u32[]{:S(2)}) collective-permute-start(bf16[320,640]{1,0:T(8,128)(2,1)S(1)} %collective-permute-done.18.refs_2_), channel_id=1, source_target_pairs={{0,4},{1,5},{2,6},{3,7},{4,0},{5,1},{6,2},{7,3},{8,12},{9,13},{10,... | collective-permute-start | bytes 1228808 | tf_op jit(solution)/shard_map/ppermute | solution.py:774
  102.2 20.4 %collective-permute-start.26 = (bf16[2,320,640]{2,1,0:T(8,128)(2,1)S(1)}, bf16[2,320,640]{2,1,0:T(8,128)(2,1)S(1)}, u32[]{:S(2)}, u32[]{:S(2)}) collective-permute-start(bf16[2,320,640]{2,1,0:T(8,128)(2,1)S(1)} %get-tuple-element.144), channel_id=1, source_target_pairs={{0,2},{1,3},{2,0},{3,1},{4,6},{5,7},{6,4},{7,5},{8,10},{9,11},{10,... | collective-permute-start | bytes 2457608 | tf_op jit(solution)/shard_map/ppermute | solution.py:774
  103.3 21.8 %collective-permute-start.27 = (bf16[2,320,640]{2,1,0:T(8,128)(2,1)S(1)}, bf16[2,320,640]{2,1,0:T(8,128)(2,1)S(1)}, u32[]{:S(2)}, u32[]{:S(2)}) collective-permute-start(bf16[2,320,640]{2,1,0:T(8,128)(2,1)S(1)} %get-tuple-element.153), channel_id=1, source_target_pairs={{0,4},{1,5},{2,6},{3,7},{4,0},{5,1},{6,2},{7,3},{8,12},{9,13},{10,... | collective-permute-start | bytes 2457608 | tf_op jit(solution)/shard_map/ppermute | solution.py:774
  123.6 22.4 %collective-permute-start.28 = (bf16[320,640]{1,0:T(8,128)(2,1)}, bf16[320,640]{1,0:T(8,128)(2,1)}, u32[]{:S(2)}, u32[]{:S(2)}) collective-permute-start(bf16[320,640]{1,0:T(8,128)(2,1)} %fusion.6), channel_id=1, source_target_pairs={{0,4},{1,5},{2,6},{3,7},{4,0},{5,1},{6,2},{7,3},{8,12},{9,13},{10,... | collective-permute-start | bytes 1228808 | tf_op jit(solution)/shard_map/ppermute | solution.py:774
  126.1 19.8 %collective-permute-start.29 = (bf16[320,640]{1,0:T(8,128)(2,1)}, bf16[320,640]{1,0:T(8,128)(2,1)}, u32[]{:S(2)}, u32[]{:S(2)}) collective-permute-start(bf16[320,640]{1,0:T(8,128)(2,1)} %fusion.7), channel_id=1, source_target_pairs={{0,2},{1,3},{2,0},{3,1},{4,6},{5,7},{6,4},{7,5},{8,10},{9,11},{10,... | collective-permute-start | bytes 1228808 | tf_op jit(solution)/shard_map/ppermute | solution.py:774
  126.7 36.4 %collective-permute-start.33 = (bf16[2,80,2560]{2,1,0:T(8,128)(2,1)}, bf16[2,80,2560]{2,1,0:T(8,128)(2,1)}, u32[]{:S(2)}, u32[]{:S(2)}) collective-permute-start(bf16[2,80,2560]{2,1,0:T(8,128)(2,1)} %get-tuple-element.180), channel_id=1, source_target_pairs={{0,2},{1,3},{2,0},{3,1},{4,6},{5,7},{6,4},{7,5},{8,10},{9,11},{10,... | collective-permute-start | bytes 2457608 | tf_op jit(solution)/shard_map/ppermute | solution.py:774
  128.2 34.9 %collective-permute-start.34 = (bf16[2,80,2560]{2,1,0:T(8,128)(2,1)}, bf16[2,80,2560]{2,1,0:T(8,128)(2,1)}, u32[]{:S(2)}, u32[]{:S(2)}) collective-permute-start(bf16[2,80,2560]{2,1,0:T(8,128)(2,1)} %get-tuple-element.181), channel_id=1, source_target_pairs={{0,4},{1,5},{2,6},{3,7},{4,0},{5,1},{6,2},{7,3},{8,12},{9,13},{10,... | collective-permute-start | bytes 2457608 | tf_op jit(solution)/shard_map/ppermute | solution.py:774
  147.2 20.2 %collective-permute-start.31 = (bf16[320,640]{1,0:T(8,128)(2,1)S(1)}, bf16[320,640]{1,0:T(8,128)(2,1)S(1)}, u32[]{:S(2)}, u32[]{:S(2)}) collective-permute-start(bf16[320,640]{1,0:T(8,128)(2,1)S(1)} %fusion.3), channel_id=1, source_target_pairs={{0,8},{24,16},{1,9},{25,17},{2,10},{26,18},{3,11},{27,19},{4,12},{... | collective-permute-start | bytes 1228808 | tf_op jit(solution)/shard_map/ppermute | solution.py:810
  151.9 15.5 %collective-permute-start.32 = (bf16[320,640]{1,0:T(8,128)(2,1)S(1)}, bf16[320,640]{1,0:T(8,128)(2,1)S(1)}, u32[]{:S(2)}, u32[]{:S(2)}) collective-permute-start(bf16[320,640]{1,0:T(8,128)(2,1)S(1)} %fusion.2), channel_id=1, source_target_pairs={{0,8},{24,16},{1,9},{25,17},{2,10},{26,18},{3,11},{27,19},{4,12},{... | collective-permute-start | bytes 1228808 | tf_op jit(solution)/shard_map/ppermute | solution.py:810
  164.2 12.4 %collective-permute-start.37 = (bf16[80,2560]{1,0:T(8,128)(2,1)S(1)}, bf16[80,2560]{1,0:T(8,128)(2,1)S(1)}, u32[]{:S(2)}, u32[]{:S(2)}) collective-permute-start(bf16[80,2560]{1,0:T(8,128)(2,1)S(1)} %fusion.8), channel_id=1, source_target_pairs={{0,4},{1,5},{2,6},{3,7},{4,0},{5,1},{6,2},{7,3},{8,12},{9,13},{10,... | collective-permute-start | bytes 1228808 | tf_op jit(solution)/shard_map/ppermute | solution.py:774
  167.7 22.1 %collective-permute-start.41 = (bf16[640,640]{1,0:T(8,128)(2,1)S(1)}, bf16[640,640]{1,0:T(8,128)(2,1)S(1)}, u32[]{:S(2)}, u32[]{:S(2)}) collective-permute-start(bf16[640,640]{1,0:T(8,128)(2,1)S(1)} %pad_maximum_fusion), channel_id=1, source_target_pairs={{8,16},{16,8},{9,17},{17,9},{10,18},{18,10},{11,19},{19,11},{12,20... | collective-permute-start | bytes 2457608 | tf_op jit(solution)/shard_map/ppermute | solution.py:810
  169.3 18.9 %collective-permute-start.35 = (bf16[2,88,1280]{2,1,0:T(8,128)(2,1)S(1)}, bf16[2,88,1280]{2,1,0:T(8,128)(2,1)S(1)}, u32[]{:S(2)}, u32[]{:S(2)}) collective-permute-start(bf16[2,88,1280]{2,1,0:T(8,128)(2,1)S(1)} %get-tuple-element.223), channel_id=1, source_target_pairs={{0,2},{1,3},{2,0},{3,1},{4,6},{5,7},{6,4},{7,5},{8,10},{9,11},{10,... | collective-permute-start | bytes 1351688 | tf_op jit(solution)/shard_map/ppermute | solution.py:774
  170.9 17.3 %collective-permute-start.36 = (bf16[2,88,1280]{2,1,0:T(8,128)(2,1)S(1)}, bf16[2,88,1280]{2,1,0:T(8,128)(2,1)S(1)}, u32[]{:S(2)}, u32[]{:S(2)}) collective-permute-start(bf16[2,88,1280]{2,1,0:T(8,128)(2,1)S(1)} %get-tuple-element.222), channel_id=1, source_target_pairs={{0,4},{1,5},{2,6},{3,7},{4,0},{5,1},{6,2},{7,3},{8,12},{9,13},{10,... | collective-permute-start | bytes 1351688 | tf_op jit(solution)/shard_map/ppermute | solution.py:774
  181.6 16.6 %collective-permute-start.43 = (bf16[80,2560]{1,0:T(8,128)(2,1)S(1)}, bf16[80,2560]{1,0:T(8,128)(2,1)S(1)}, u32[]{:S(2)}, u32[]{:S(2)}) collective-permute-start(bf16[80,2560]{1,0:T(8,128)(2,1)S(1)} %fusion.1), channel_id=1, source_target_pairs={{0,8},{24,16},{1,9},{25,17},{2,10},{26,18},{3,11},{27,19},{4,12},{... | collective-permute-start | bytes 1228808 | tf_op jit(solution)/shard_map/ppermute | solution.py:810
  182.9 18.6 %collective-permute-start.45 = (bf16[80,2560]{1,0:T(8,128)(2,1)S(1)}, bf16[80,2560]{1,0:T(8,128)(2,1)S(1)}, u32[]{:S(2)}, u32[]{:S(2)}) collective-permute-start(bf16[80,2560]{1,0:T(8,128)(2,1)S(1)} %fusion), channel_id=1, source_target_pairs={{0,8},{24,16},{1,9},{25,17},{2,10},{26,18},{3,11},{27,19},{4,12},{... | collective-permute-start | bytes 1228808 | tf_op jit(solution)/shard_map/ppermute | solution.py:810
  190.1 23.0 %collective-permute-start.54 = (bf16[640,640]{1,0:T(8,128)(2,1)S(1)}, bf16[640,640]{1,0:T(8,128)(2,1)S(1)}, u32[]{:S(2)}, u32[]{:S(2)}) collective-permute-start(bf16[640,640]{1,0:T(8,128)(2,1)S(1)} %add_convert_fusion.1), channel_id=1, source_target_pairs={{8,0},{16,24},{9,1},{17,25},{10,2},{18,26},{11,3},{19,27},{12,4},{... | collective-permute-start | bytes 2457608 | tf_op jit(solution)/shard_map/ppermute | solution.py:810
  202.4 19.4 %collective-permute-start.52 = (bf16[80,2560]{1,0:T(8,128)(2,1)S(1)}, bf16[80,2560]{1,0:T(8,128)(2,1)S(1)}, u32[]{:S(2)}, u32[]{:S(2)}) collective-permute-start(bf16[80,2560]{1,0:T(8,128)(2,1)S(1)} %add_convert_fusion.3), channel_id=1, source_target_pairs={{8,0},{16,24},{9,1},{17,25},{10,2},{18,26},{11,3},{19,27},{12,4},{... | collective-permute-start | bytes 1228808 | tf_op jit(solution)/shard_map/ppermute | solution.py:810
  207.2 24.9 %collective-permute-start.53 = (bf16[80,2560]{1,0:T(8,128)(2,1)S(1)}, bf16[80,2560]{1,0:T(8,128)(2,1)S(1)}, u32[]{:S(2)}, u32[]{:S(2)}) collective-permute-start(bf16[80,2560]{1,0:T(8,128)(2,1)S(1)} %add_convert_fusion.2), channel_id=1, source_target_pairs={{8,0},{16,24},{9,1},{17,25},{10,2},{18,26},{11,3},{19,27},{12,4},{... | collective-permute-start | bytes 1228808 | tf_op jit(solution)/shard_map/ppermute | solution.py:810
  209.9 25.8 %collective-permute-start.50 = (bf16[88,1280]{1,0:T(8,128)(2,1)S(1)}, bf16[88,1280]{1,0:T(8,128)(2,1)S(1)}, u32[]{:S(2)}, u32[]{:S(2)}) collective-permute-start(bf16[88,1280]{1,0:T(8,128)(2,1)S(1)} %add_convert_fusion.13.refs_0_), channel_id=1, source_target_pairs={{8,0},{16,24},{9,1},{17,25},{10,2},{18,26},{11,3},{19,27},{12,4},{... | collective-permute-start | bytes 675848 | tf_op jit(solution)/shard_map/ppermute | solution.py:810
  211.3 26.9 %collective-permute-start.51 = (bf16[88,1280]{1,0:T(8,128)(2,1)S(1)}, bf16[88,1280]{1,0:T(8,128)(2,1)S(1)}, u32[]{:S(2)}, u32[]{:S(2)}) collective-permute-start(bf16[88,1280]{1,0:T(8,128)(2,1)S(1)} %add_convert_fusion.12.refs_1_), channel_id=1, source_target_pairs={{8,0},{16,24},{9,1},{17,25},{10,2},{18,26},{11,3},{19,27},{12,4},{... | collective-permute-start | bytes 675848 | tf_op jit(solution)/shard_map/ppermute | solution.py:810
  (72 other events, 586.0 us)
where the time goes:
time: 242 us
  waiting for transfers between devices  88.7 us (37%)
  Pallas kernels  81.1 us (34%)
  starting transfers between devices  51 us (21%)
  other arithmetic  12.3 us (5%)
  local copies, waits for them, and re-layouts  6.83 us (3%)
    pallas_call x16, Pallas kernels, call(): pl.pallas_call(kernel, out_shape=shapes, grid_spec=pltpu.PrefetchScalarGr...  81.1 us
    ppermute x40, waiting for transfers between devices, swap(): lax.ppermute(values, 'wide', [(i, i ^ bit) for i in range(lax.axis_size('...  58.9 us
    ppermute x40, starting transfers between devices, swap(): lax.ppermute(values, 'wide', [(i, i ^ bit) for i in range(lax.axis_size('...  30.8 us
    ppermute x16, waiting for transfers between devices, hop(): return [lax.ppermute(part, 'narrow', pairs) for part in parts]  29.8 us
    ppermute x16, starting transfers between devices, hop(): return [lax.ppermute(part, 'narrow', pairs) for part in parts]  20.2 us
    convert_element_type x21, other arithmetic, add_low(): return sum((part.astype(F32) for part in parts)).astype(BF16)  10.7 us
  transfers between devices with their start and end apart: 56, of which 26 were waited for; matrix products, arithmetic and copies ran while one was open for 6% of the time, Pallas kernels for 30%

commit v1 on v0

--- a/solution.py
+++ b/solution.py
@@ -298,24 +298,35 @@
     )
 
 
-def slab_kernel(heads_ref, out_ref, short_ref, up_ref, slab_ref):
-    rows = heads_ref.shape[0]
-    width = out_ref.shape[1]
-    slab_ref[:rows, : 3 * width] = heads_ref[...]
-    slab_ref[:rows, 3 * width :] = out_ref[...]
+def slab_kernel(heads_far, out_far, short_ref, up_ref, slab_ref, sems):
+    rows = heads_far.shape[0]
+    width = out_far.shape[1]
+    copies = [
+        pltpu.make_async_copy(far, slab_ref.at[pl.ds(0, rows), here], sems.at[at])
+        for at, (far, here) in enumerate(
+            ((heads_far, pl.ds(0, 3 * width)), (out_far, pl.ds(3 * width, width)))
+        )
+    ]
+    for copy in copies:
+        copy.start()
     slab_ref[rows:, :] = jnp.zeros((VECTORS, 4 * width), BF16)
     slab_ref[rows:, :rows] = short_ref[...]
     slab_ref[rows:, LANES : LANES + up_ref.shape[1]] = jnp.broadcast_to(
         up_ref[...], (VECTORS, up_ref.shape[1])
     )
-
-
-def project_kernel(count, rows, hidden, position_ref, x_ref, *refs):
+    for copy in copies:
+        copy.wait()
+
+
+def project_kernel(count, rows, hidden, position_ref, x_far, *refs):
     slabs, refs = refs[:count], refs[count:]
-    length, width = x_ref.shape
+    length, width = x_far.shape
+    x_ref = x_far
     if count:
-        low_ref, joined_ref, heads_ref, out_ref, vector_ref, bias_ref, short_ref, sems = refs
-        copies = []
+        low_ref, joined_ref, heads_ref, out_ref, vector_ref, bias_ref, *refs = refs
+        short_ref, x_ref, sems, x_sem = refs
+        copies = [pltpu.make_async_copy(x_far, x_ref, x_sem)]
+        copies[0].start()
         for at, slab in enumerate(slabs):
             begin = pl.multiple_of(position_ref[at] * rows, SUBLANES)
             here = pl.ds(begin, rows)
@@ -868,6 +879,8 @@
             slab_kernel,
             [((rows + VECTORS, 4 * width), BF16)],
             (heads_weight, output_weight, short, up_bias[None]),
+            in_specs=[far_away, far_away, vmem, vmem],
+            scratch=[pltpu.SemaphoreType.DMA((2,))],
         )
         near_x, near_y, far = swap(slab, 2), swap(slab, 4), swap(slab, 6)
         swapped = swap(slab, 1)
@@ -886,11 +899,12 @@
             ],
             (x, *slabs),
             positions,
-            in_specs=[pl.BlockSpec(memory_space=pltpu.VMEM)]
-            + [pl.BlockSpec(memory_space=pltpu.HBM)] * len(slabs),
+            in_specs=[far_away] * (1 + len(slabs)),
             scratch=[
                 pltpu.VMEM((len(slabs), VECTORS, LANES + hidden), BF16),
+                pltpu.VMEM((length, width), BF16),
                 pltpu.SemaphoreType.DMA((len(slabs), 3)),
+                pltpu.SemaphoreType.DMA,
             ],
             mib=20,
         )

time: 242 us -> 242 us (level)
  local copies, waits for them, and re-layouts: 6.83 us -> 3.81 us
    unnamed x96 -> x86, local copies, waits for them, and re-layouts: 4.01 us -> 1 us
  transfers between devices with their start and end apart: 56 -> 56, of which waited for: 26 -> 26; matrix products, arithmetic and copies ran while one was open for 6% -> 6% of each run, Pallas kernels for 30% -> 31%
where the time goes in v1:
time: 242 us; the launch traced here: 241 us
  waiting for transfers between devices  88.7 us (37%)
  Pallas kernels  83.5 us (35%)
  starting transfers between devices  50.9 us (21%)
  other arithmetic  12.3 us (5%)
  local copies, waits for them, and re-layouts  3.81 us (2%)
    pallas_call x16, Pallas kernels, call(): pl.pallas_call(kernel, out_shape=shapes, grid_spec=pltpu.PrefetchScalarGr...  83.5 us
    ppermute x40, waiting for transfers between devices, swap(): lax.ppermute(values, 'wide', [(i, i ^ bit) for i in range(lax.axis_size('...  59.2 us
    ppermute x40, starting transfers between devices, swap(): lax.ppermute(values, 'wide', [(i, i ^ bit) for i in range(lax.axis_size('...  30.7 us
    ppermute x16, waiting for transfers between devices, hop(): return [lax.ppermute(part, 'narrow', pairs) for part in parts]  29.5 us
    ppermute x16, starting transfers between devices, hop(): return [lax.ppermute(part, 'narrow', pairs) for part in parts]  20.2 us
    convert_element_type x21, other arithmetic, add_low(): return sum((part.astype(F32) for part in parts)).astype(BF16)  10.7 us
  transfers between devices with their start and end apart: 56, of which 26 were waited for; matrix products, arithmetic and copies ran while one was open for 6% of the time, Pallas kernels for 31%

profile of v1, /device:TPU:0, one launch (start us, length us, event | category | flops | bytes accessed | tf_op | source)
XLA Modules:
  0.0 240.9 jit_solution(7579961604267940354)
XLA Ops:
  3.2 3.0 %collective-permute-start = (bf16[88,2560]{1,0:T(8,128)(2,1)S(1)}, bf16[88,2560]{1,0:T(8,128)(2,1)S(1)}, u32[]{:S(2)}, u32[]{:S(2)}) collective-permute-start(bf16[88,2560]{1,0:T(8,128)(2,1)S(1)} %shard_map.305.refs_0_), channel_id=1, source_target_pairs={{0,2},{1,3},{2,0},{3,1},{4,6},{5,7},{6,4},{7,5},{8,10},{9,11},{10,... | collective-permute-start | bytes 1351688 | tf_op jit(solution)/shard_map/ppermute | solution.py:785
  7.8 9.6 %collective-permute-done.refs_1_ = bf16[88,2560]{1,0:T(8,128)(2,1)S(1)} collective-permute-done((bf16[88,2560]{1,0:T(8,128)(2,1)S(1)}, bf16[88,2560]{1,0:T(8,128)(2,1)S(1)}, u32[]{:S(2)}, u32[]{:S(2)}) %collective-permute-start) | collective-permute-done | bytes 450592 | tf_op jit(solution)/shard_map/ppermute | solution.py:785
  17.5 2.1 collective-permute-start.7
  21.1 8.0 %collective-permute-done.2.refs_2_ = bf16[88,2560]{1,0:T(8,128)(2,1)S(1)} collective-permute-done((bf16[88,2560]{1,0:T(8,128)(2,1)S(1)}, bf16[88,2560]{1,0:T(8,128)(2,1)S(1)}, u32[]{:S(2)}, u32[]{:S(2)}) %collective-permute-start.2) | collective-permute-done | bytes 450592 | tf_op jit(solution)/shard_map/ppermute | solution.py:785
  32.4 5.2 %shard_map.306 = (bf16[512,640]{1,0:T(8,128)(2,1)S(1)}, bf16[512,1920]{1,0:T(8,128)(2,1)S(1)}, bf16[640,1920]{1,0:T(8,128)(2,1)S(1)}, bf16[640,640]{1,0:T(8,128)...) custom-call(s32[8]{0:T(128)S(1)} %pad_add_fusion.position_ref, bf16[512,640]{1,0:T(8,128)(2,1)} %bitcast.69, ...), custom_call_target="tpu_custom_call" | custom-call | flops 1 | bytes 1 | tf_op jit(solution)/shard_map/pallas_call | solution.py:56
  37.7 7.9 %shard_map.307 = (bf16[512,640]{1,0:T(8,128)(2,1)S(1)}, f32[640,512]{1,0:T(8,128)S(1)}, f32[40,512]{1,0:T(8,128)S(1)}) custom-call(s32[1,512]{1,0:T(1,128)S(1)} %copy-done.26, bf16[512,1920]{1,0:T(8,128)(2,1)S(1)} %get-tuple-element.118.q_ref.k_ref.v_ref, bf16[512,1920]{1,0:T(8,128)(2,1)S(1)} %get-tuple-element.118.q_ref.k_ref.v_ref, ...), custom_call_target="tpu_custom_call" | custom-call | flops 1 | bytes 1 | tf_op jit(solution)/shard_map/pallas_call | solution.py:56
  50.3 7.9 %collective-permute-done.13.refs_3_ = bf16[40,5120]{1,0:T(8,128)(2,1)S(1)} collective-permute-done((bf16[40,5120]{1,0:T(8,128)(2,1)S(1)}, bf16[40,5120]{1,0:T(8,128)(2,1)S(1)}, u32[]{:S(2)}, u32[]{:S(2)}) %collective-permute-start.13) | collective-permute-done | bytes 409632 | tf_op jit(solution)/shard_map/ppermute | solution.py:785
  62.8 9.5 %shard_map.309 = (bf16[1024,2560]{1,0:T(8,128)(2,1)S(1)}, bf16[1024,2560]{1,0:T(8,128)(2,1)S(1)}, bf16[640,2560]{1,0:T(8,128)(2,1)S(1)}) custom-call(s32[11]{0:T(128)S(1)} %compare_select_fusion.1.position_ref, bf16[512,640]{1,0:T(8,128)(2,1)S(1)} %get-tuple-element.128.own_ref.second_ref, ...), custom_call_target="tpu_custom_call" | custom-call | flops 1 | bytes 1 | tf_op jit(solution)/shard_map/pallas_call | solution.py:56
  75.3 4.5 %collective-permute-done.17.refs_1_ = bf16[320,640]{1,0:T(8,128)(2,1)S(1)} collective-permute-done((bf16[320,640]{1,0:T(8,128)(2,1)S(1)}, bf16[320,640]{1,0:T(8,128)(2,1)S(1)}, u32[]{:S(2)}, u32[]{:S(2)}) %collective-permute-start.17) | collective-permute-done | bytes 409632 | tf_op jit(solution)/shard_map/ppermute | solution.py:785
  81.1 4.4 %shard_map.310 = (f32[1024,640]{1,0:T(8,128)S(1)}, bf16[2560,640]{1,0:T(8,128)(2,1)S(1)}) custom-call(s32[7]{0:T(128)S(1)} %compare_select_fusion.2.position_ref, bf16[1024,2560]{1,0:T(8,128)(2,1)S(1)} %get-tuple-element.130.act_ref, bf16[640,640]{1,0:T(8,128)(2,1)S(1)} %copy-done.2, bf16[320,640]{1,0:T(8,128)(2,1)S(1)} %collective-permute-done.17.refs_1_, ...), custom_call_target="tpu_custom_call" | custom-call | flops 1 | bytes 1 | tf_op jit(solution)/shard_map/pallas_call | solution.py:56
  85.5 2.6 %collective-permute-done.21.upper_ref = bf16[320,640]{1,0:T(8,128)(2,1)S(1)} collective-permute-done((bf16[320,640]{1,0:T(8,128)(2,1)S(1)}, bf16[320,640]{1,0:T(8,128)(2,1)S(1)}, u32[]{:S(2)}, u32[]{:S(2)}) %collective-permute-start.21) | collective-permute-done | bytes 409632 | tf_op jit(solution)/shard_map/ppermute | solution.py:785
  89.2 1.9 shard_map.311
  91.1 2.1 collective-permute-done.23.got_ref
  94.5 2.0 collective-permute-done.24.other_ref
  96.5 4.3 %shard_map.313 = (bf16[2,320,640]{2,1,0:T(8,128)(2,1)S(1)}, bf16[2,320,640]{2,1,0:T(8,128)(2,1)S(1)}, bf16[2,320,640]{2,1,0:T(8,128)(2,1)S(1)}, bf16[2,320,640]{2,1,0:T(8,128)(2,1)S(1)}) custom-call(s32[1]{0:T(128)} %bitcast.11.position_ref, bf16[1024,2560]{1,0:T(8,128)(2,1)S(1)} %get-tuple-element.130.act_ref, ...), custom_call_target="tpu_custom_call" | custom-call | flops 1 | bytes 1 | tf_op jit(solution)/shard_map/pallas_call | solution.py:56
  102.9 10.9 %shard_map.314 = (bf16[1024,2560]{1,0:T(8,128)(2,1)S(1)}, f32[1,2560]{1,0:T(1,128)S(1)}, bf16[2,80,2560]{2,1,0:T(8,128)(2,1)S(1)}, bf16[2,80,2560]{2,1,0:T(8,128...) custom-call(s32[1]{0:T(128)} %bitcast.11.position_ref, ...), custom_call_target="tpu_custom_call" | custom-call | flops 1 | bytes 1 | tf_op jit(solution)/shard_map/pallas_call | solution.py:56
  113.8 6.0 %shard_map.315 = (f32[512,640]{1,0:T(8,128)}, bf16[512,640]{1,0:T(8,128)(2,1)}) custom-call(bf16[1024,2560]{1,0:T(8,128)(2,1)S(1)} %get-tuple-element.148.grad_ref, bf16[640,2560]{1,0:T(8,128)(2,1)S(1)} %get-tuple-element.149.up_ref), custom_call_target="tpu_custom_call" | custom-call | flops 1 | bytes 1 | tf_op jit(solution)/shard_map/pallas_call | solution.py:56
  127.2 5.1 %shard_map.316 = (f32[512,640]{1,0:T(8,128)S(1)}, bf16[512,640]{1,0:T(8,128)(2,1)S(1)}, bf16[512,640]{1,0:T(8,128)(2,1)S(1)}, f32[8,640]{1,0:T(8,128)S(1)}) custom-call(bf16[512,640]{1,0:T(8,128)(2,1)} %collective-permute-done.25.got_ref, f32[512,640]{1,0:T(8,128)} %get-tuple-element.155.own_far, f32[512,640]{1,0:T(8,128)} %copy-done.1, ...), custom_call_target="tpu_custom_call" | custom-call | flops 1 | bytes 1 | tf_op jit(solution)/shard_map/pallas_call | solution.py:56
  132.5 13.0 %shard_map.317 = (bf16[512,640]{1,0:T(8,128)(2,1)S(1)}, bf16[512,640]{1,0:T(8,128)(2,1)S(1)}, bf16[512,640]{1,0:T(8,128)(2,1)S(1)}) custom-call(s32[1,512]{1,0:T(1,128)S(1)} %copy-done.27, bf16[512,1920]{1,0:T(8,128)(2,1)S(1)} %get-tuple-element.118.q_ref.k_ref.v_ref, bf16[512,1920]{1,0:T(8,128)(2,1)S(1)} %get-tuple-element.118.q_ref.k_ref.v_ref, ...), custom_call_target="tpu_custom_call" | custom-call | flops 1 | bytes 1 | tf_op jit(solution)/shard_map/pallas_call | solution.py:56
  146.9 3.5 %collective-permute-start.31 = (bf16[320,640]{1,0:T(8,128)(2,1)S(1)}, bf16[320,640]{1,0:T(8,128)(2,1)S(1)}, u32[]{:S(2)}, u32[]{:S(2)}) collective-permute-start(bf16[320,640]{1,0:T(8,128)(2,1)S(1)} %fusion.3), channel_id=1, source_target_pairs={{0,8},{24,16},{1,9},{25,17},{2,10},{26,18},{3,11},{27,19},{4,12},{... | collective-permute-start | bytes 1228808 | tf_op jit(solution)/shard_map/ppermute | solution.py:821
  152.9 9.7 %shard_map.318 = (bf16[8,88,1280]{2,1,0:T(8,128)(2,1)S(1)}, bf16[8,88,1280]{2,1,0:T(8,128)(2,1)S(1)}, f32[512,640]{1,0:T(8,128)}, f32[8,640]{1,0:T(8,128)}, bf16[640,2560]{1,0:T(8,128)(2,1)}) custom-call(s32[8]{0:T(128)S(1)} %copy-done.31, bf16[512,640]{1,0:T(8,128)(2,1)S(1)} %bitcast.71, bf16[512,640]{1,0:T(8,128)(2,1)S(1)} %copy-done.20, ...), custom_call_target="tpu_custom_call" | custom-call | flops 1 | bytes 1 | tf_op jit(solution)/shard_map/pallas_call | solution.py:56
  163.8 1.6 collective-permute-start.37
  171.0 5.2 %collective-permute-done.37 = bf16[80,2560]{1,0:T(8,128)(2,1)S(1)} collective-permute-done((bf16[80,2560]{1,0:T(8,128)(2,1)S(1)}, bf16[80,2560]{1,0:T(8,128)(2,1)S(1)}, u32[]{:S(2)}, u32[]{:S(2)}) %collective-permute-start.37) | collective-permute-done | bytes 409632 | tf_op jit(solution)/shard_map/ppermute | solution.py:785
  176.2 2.7 %collective-permute-done.38 = bf16[80,2560]{1,0:T(8,128)(2,1)S(1)} collective-permute-done((bf16[80,2560]{1,0:T(8,128)(2,1)S(1)}, bf16[80,2560]{1,0:T(8,128)(2,1)S(1)}, u32[]{:S(2)}, u32[]{:S(2)}) %collective-permute-start.38) | collective-permute-done | bytes 409632 | tf_op jit(solution)/shard_map/ppermute | solution.py:785
  183.9 4.0 %collective-permute-done.35 = bf16[2,88,1280]{2,1,0:T(8,128)(2,1)S(1)} collective-permute-done((bf16[2,88,1280]{2,1,0:T(8,128)(2,1)S(1)}, bf16[2,88,1280]{2,1,0:T(8,128)(2,1)S(1)}, u32[]{:S(2)}, u32[]{:S(2)}) %collective-permute-start.35) | collective-permute-done | bytes 450592 | tf_op jit(solution)/shard_map/ppermute | solution.py:785
  190.7 4.1 %collective-permute-done.39 = bf16[88,1280]{1,0:T(8,128)(2,1)S(1)} collective-permute-done((bf16[88,1280]{1,0:T(8,128)(2,1)S(1)}, bf16[88,1280]{1,0:T(8,128)(2,1)S(1)}, u32[]{:S(2)}, u32[]{:S(2)}) %collective-permute-start.39) | collective-permute-done | bytes 225312 | tf_op jit(solution)/shard_map/ppermute | solution.py:785
  198.6 2.5 %collective-permute-done.45 = bf16[80,2560]{1,0:T(8,128)(2,1)S(1)} collective-permute-done((bf16[80,2560]{1,0:T(8,128)(2,1)S(1)}, bf16[80,2560]{1,0:T(8,128)(2,1)S(1)}, u32[]{:S(2)}, u32[]{:S(2)}) %collective-permute-start.45) | collective-permute-done | bytes 409632 | tf_op jit(solution)/shard_map/ppermute | solution.py:821
  203.3 2.6 %collective-permute-done.42 = bf16[88,1280]{1,0:T(8,128)(2,1)S(1)} collective-permute-done((bf16[88,1280]{1,0:T(8,128)(2,1)S(1)}, bf16[88,1280]{1,0:T(8,128)(2,1)S(1)}, u32[]{:S(2)}, u32[]{:S(2)}) %collective-permute-start.42) | collective-permute-done | bytes 225312 | tf_op jit(solution)/shard_map/ppermute | solution.py:821
  213.5 7.4 %collective-permute-done.52 = bf16[80,2560]{1,0:T(8,128)(2,1)S(1)} collective-permute-done((bf16[80,2560]{1,0:T(8,128)(2,1)S(1)}, bf16[80,2560]{1,0:T(8,128)(2,1)S(1)}, u32[]{:S(2)}, u32[]{:S(2)}) %collective-permute-start.52) | collective-permute-done | bytes 409632 | tf_op jit(solution)/shard_map/ppermute | solution.py:821
  220.9 10.8 %collective-permute-done.53 = bf16[80,2560]{1,0:T(8,128)(2,1)S(1)} collective-permute-done((bf16[80,2560]{1,0:T(8,128)(2,1)S(1)}, bf16[80,2560]{1,0:T(8,128)(2,1)S(1)}, u32[]{:S(2)}, u32[]{:S(2)}) %collective-permute-start.53) | collective-permute-done | bytes 409632 | tf_op jit(solution)/shard_map/ppermute | solution.py:821
  231.7 3.4 %collective-permute-done.50.refs_2_ = bf16[88,1280]{1,0:T(8,128)(2,1)S(1)} collective-permute-done((bf16[88,1280]{1,0:T(8,128)(2,1)S(1)}, bf16[88,1280]{1,0:T(8,128)(2,1)S(1)}, u32[]{:S(2)}, u32[]{:S(2)}) %collective-permute-start.50) | collective-permute-done | bytes 225312 | tf_op jit(solution)/shard_map/ppermute | solution.py:821
  235.3 2.2 collective-permute-done.51.refs_3_
  (219 shorter events, 69.7 us)
Async XLA Ops:
  3.2 14.2 %collective-permute-start = (bf16[88,2560]{1,0:T(8,128)(2,1)S(1)}, bf16[88,2560]{1,0:T(8,128)(2,1)S(1)}, u32[]{:S(2)}, u32[]{:S(2)}) collective-permute-start(bf16[88,2560]{1,0:T(8,128)(2,1)S(1)} %shard_map.305.refs_0_), channel_id=1, source_target_pairs={{0,2},{1,3},{2,0},{3,1},{4,6},{5,7},{6,4},{7,5},{8,10},{9,11},{10,... | collective-permute-start | bytes 1351688 | tf_op jit(solution)/shard_map/ppermute | solution.py:785
  6.2 22.9 %collective-permute-start.2 = (bf16[88,2560]{1,0:T(8,128)(2,1)S(1)}, bf16[88,2560]{1,0:T(8,128)(2,1)S(1)}, u32[]{:S(2)}, u32[]{:S(2)}) collective-permute-start(bf16[88,2560]{1,0:T(8,128)(2,1)S(1)} %shard_map.305.refs_0_), channel_id=1, source_target_pairs={{0,4},{1,5},{2,6},{3,7},{4,0},{5,1},{6,2},{7,3},{8,12},{9,13},{10,... | collective-permute-start | bytes 1351688 | tf_op jit(solution)/shard_map/ppermute | solution.py:785
  7.7 21.4 %collective-permute-start.3 = (bf16[88,2560]{1,0:T(8,128)(2,1)S(1)}, bf16[88,2560]{1,0:T(8,128)(2,1)S(1)}, u32[]{:S(2)}, u32[]{:S(2)}) collective-permute-start(bf16[88,2560]{1,0:T(8,128)(2,1)S(1)} %shard_map.305.refs_0_), channel_id=1, source_target_pairs={{0,6},{1,7},{2,4},{3,5},{4,2},{5,3},{6,0},{7,1},{8,14},{9,15},{10,... | collective-permute-start | bytes 1351688 | tf_op jit(solution)/shard_map/ppermute | solution.py:785
  17.5 28.2 %collective-permute-start.7 = (bf16[80,5120]{1,0:T(8,128)(2,1)}, bf16[80,5120]{1,0:T(8,128)(2,1)S(1)}, u32[]{:S(2)}, u32[]{:S(2)}) collective-permute-start(bf16[80,5120]{1,0:T(8,128)(2,1)} %refs_0_.1), channel_id=1, source_target_pairs={{0,2},{1,3},{2,0},{3,1},{4,6},{5,7},{6,4},{7,5},{8,10},{9,11},{10,... | collective-permute-start | bytes 2457608 | tf_op jit(solution)/shard_map/ppermute | solution.py:785
  19.5 26.6 %collective-permute-start.8 = (bf16[80,5120]{1,0:T(8,128)(2,1)}, bf16[80,5120]{1,0:T(8,128)(2,1)S(1)}, u32[]{:S(2)}, u32[]{:S(2)}) collective-permute-start(bf16[80,5120]{1,0:T(8,128)(2,1)} %refs_0_.1), channel_id=1, source_target_pairs={{0,4},{1,5},{2,6},{3,7},{4,0},{5,1},{6,2},{7,3},{8,12},{9,13},{10,... | collective-permute-start | bytes 2457608 | tf_op jit(solution)/shard_map/ppermute | solution.py:785
  29.7 20.4 %collective-permute-start.9 = (bf16[80,5120]{1,0:T(8,128)(2,1)}, bf16[80,5120]{1,0:T(8,128)(2,1)S(1)}, u32[]{:S(2)}, u32[]{:S(2)}) collective-permute-start(bf16[80,5120]{1,0:T(8,128)(2,1)} %refs_0_.1), channel_id=1, source_target_pairs={{0,1},{1,0},{2,3},{3,2},{4,5},{5,4},{6,7},{7,6},{8,9},{9,8},{10,11... | collective-permute-start | bytes 2457608 | tf_op jit(solution)/shard_map/ppermute | solution.py:785
  50.1 12.7 %collective-permute-start.12 = (bf16[512,640]{1,0:T(8,128)(2,1)S(1)}, bf16[512,640]{1,0:T(8,128)(2,1)S(1)}, u32[]{:S(2)}, u32[]{:S(2)}) collective-permute-start(bf16[512,640]{1,0:T(8,128)(2,1)S(1)} %get-tuple-element.128.own_ref.second_ref), channel_id=1, source_target_pairs={{0,1},{1,0},{2,3},{3,2},{4,5},{5,4},{6,7},{7,6},{8,9},{9,8},{10,11... | collective-permute-start | bytes 1966088 | tf_op jit(solution)/shard_map/ppermute | solution.py:785
  58.7 13.7 %collective-permute-start.18 = (bf16[320,640]{1,0:T(8,128)(2,1)S(1)}, bf16[320,640]{1,0:T(8,128)(2,1)S(1)}, u32[]{:S(2)}, u32[]{:S(2)}) collective-permute-start(bf16[320,640]{1,0:T(8,128)(2,1)S(1)} %get-tuple-element.132), channel_id=1, source_target_pairs={{0,2},{1,3},{2,0},{3,1},{4,6},{5,7},{6,4},{7,5},{8,10},{9,11},{10,... | collective-permute-start | bytes 1228808 | tf_op jit(solution)/shard_map/ppermute | solution.py:785
  61.5 18.2 %collective-permute-start.17 = (bf16[320,640]{1,0:T(8,128)(2,1)S(1)}, bf16[320,640]{1,0:T(8,128)(2,1)S(1)}, u32[]{:S(2)}, u32[]{:S(2)}) collective-permute-start(bf16[320,640]{1,0:T(8,128)(2,1)S(1)} %get-tuple-element.131), channel_id=1, source_target_pairs={{0,2},{1,3},{2,0},{3,1},{4,6},{5,7},{6,4},{7,5},{8,10},{9,11},{10,... | collective-permute-start | bytes 1228808 | tf_op jit(solution)/shard_map/ppermute | solution.py:785
  62.3 18.8 %collective-permute-start.20 = (bf16[320,640]{1,0:T(8,128)(2,1)S(1)}, bf16[320,640]{1,0:T(8,128)(2,1)S(1)}, u32[]{:S(2)}, u32[]{:S(2)}) collective-permute-start(bf16[320,640]{1,0:T(8,128)(2,1)S(1)} %get-tuple-element.132), channel_id=1, source_target_pairs={{0,4},{1,5},{2,6},{3,7},{4,0},{5,1},{6,2},{7,3},{8,12},{9,13},{10,... | collective-permute-start | bytes 1228808 | tf_op jit(solution)/shard_map/ppermute | solution.py:785
  72.4 15.7 %collective-permute-start.21 = (bf16[320,640]{1,0:T(8,128)(2,1)S(1)}, bf16[320,640]{1,0:T(8,128)(2,1)S(1)}, u32[]{:S(2)}, u32[]{:S(2)}) collective-permute-start(bf16[320,640]{1,0:T(8,128)(2,1)S(1)} %collective-permute-done.19.refs_3_), channel_id=1, source_target_pairs={{0,2},{1,3},{2,0},{3,1},{4,6},{5,7},{6,4},{7,5},{8,10},{9,11},{10,... | collective-permute-start | bytes 1228808 | tf_op jit(solution)/shard_map/ppermute | solution.py:785
  73.8 15.4 %collective-permute-start.22 = (bf16[320,640]{1,0:T(8,128)(2,1)S(1)}, bf16[320,640]{1,0:T(8,128)(2,1)S(1)}, u32[]{:S(2)}, u32[]{:S(2)}) collective-permute-start(bf16[320,640]{1,0:T(8,128)(2,1)S(1)} %collective-permute-done.18.refs_2_), channel_id=1, source_target_pairs={{0,4},{1,5},{2,6},{3,7},{4,0},{5,1},{6,2},{7,3},{8,12},{9,13},{10,... | collective-permute-start | bytes 1228808 | tf_op jit(solution)/shard_map/ppermute | solution.py:785
  100.8 20.4 %collective-permute-start.26 = (bf16[2,320,640]{2,1,0:T(8,128)(2,1)S(1)}, bf16[2,320,640]{2,1,0:T(8,128)(2,1)S(1)}, u32[]{:S(2)}, u32[]{:S(2)}) collective-permute-start(bf16[2,320,640]{2,1,0:T(8,128)(2,1)S(1)} %get-tuple-element.144), channel_id=1, source_target_pairs={{0,2},{1,3},{2,0},{3,1},{4,6},{5,7},{6,4},{7,5},{8,10},{9,11},{10,... | collective-permute-start | bytes 2457608 | tf_op jit(solution)/shard_map/ppermute | solution.py:785
  101.5 22.1 %collective-permute-start.27 = (bf16[2,320,640]{2,1,0:T(8,128)(2,1)S(1)}, bf16[2,320,640]{2,1,0:T(8,128)(2,1)S(1)}, u32[]{:S(2)}, u32[]{:S(2)}) collective-permute-start(bf16[2,320,640]{2,1,0:T(8,128)(2,1)S(1)} %get-tuple-element.153), channel_id=1, source_target_pairs={{0,4},{1,5},{2,6},{3,7},{4,0},{5,1},{6,2},{7,3},{8,12},{9,13},{10,... | collective-permute-start | bytes 2457608 | tf_op jit(solution)/shard_map/ppermute | solution.py:785
  122.1 23.4 %collective-permute-start.28 = (bf16[320,640]{1,0:T(8,128)(2,1)}, bf16[320,640]{1,0:T(8,128)(2,1)}, u32[]{:S(2)}, u32[]{:S(2)}) collective-permute-start(bf16[320,640]{1,0:T(8,128)(2,1)} %fusion.6), channel_id=1, source_target_pairs={{0,4},{1,5},{2,6},{3,7},{4,0},{5,1},{6,2},{7,3},{8,12},{9,13},{10,... | collective-permute-start | bytes 1228808 | tf_op jit(solution)/shard_map/ppermute | solution.py:785
  124.7 20.8 %collective-permute-start.29 = (bf16[320,640]{1,0:T(8,128)(2,1)}, bf16[320,640]{1,0:T(8,128)(2,1)}, u32[]{:S(2)}, u32[]{:S(2)}) collective-permute-start(bf16[320,640]{1,0:T(8,128)(2,1)} %fusion.7), channel_id=1, source_target_pairs={{0,2},{1,3},{2,0},{3,1},{4,6},{5,7},{6,4},{7,5},{8,10},{9,11},{10,... | collective-permute-start | bytes 1228808 | tf_op jit(solution)/shard_map/ppermute | solution.py:785
  125.2 37.5 %collective-permute-start.33 = (bf16[2,80,2560]{2,1,0:T(8,128)(2,1)}, bf16[2,80,2560]{2,1,0:T(8,128)(2,1)}, u32[]{:S(2)}, u32[]{:S(2)}) collective-permute-start(bf16[2,80,2560]{2,1,0:T(8,128)(2,1)} %get-tuple-element.180), channel_id=1, source_target_pairs={{0,2},{1,3},{2,0},{3,1},{4,6},{5,7},{6,4},{7,5},{8,10},{9,11},{10,... | collective-permute-start | bytes 2457608 | tf_op jit(solution)/shard_map/ppermute | solution.py:785
  126.7 36.0 %collective-permute-start.34 = (bf16[2,80,2560]{2,1,0:T(8,128)(2,1)}, bf16[2,80,2560]{2,1,0:T(8,128)(2,1)}, u32[]{:S(2)}, u32[]{:S(2)}) collective-permute-start(bf16[2,80,2560]{2,1,0:T(8,128)(2,1)} %get-tuple-element.181), channel_id=1, source_target_pairs={{0,4},{1,5},{2,6},{3,7},{4,0},{5,1},{6,2},{7,3},{8,12},{9,13},{10,... | collective-permute-start | bytes 2457608 | tf_op jit(solution)/shard_map/ppermute | solution.py:785
  146.9 20.2 %collective-permute-start.31 = (bf16[320,640]{1,0:T(8,128)(2,1)S(1)}, bf16[320,640]{1,0:T(8,128)(2,1)S(1)}, u32[]{:S(2)}, u32[]{:S(2)}) collective-permute-start(bf16[320,640]{1,0:T(8,128)(2,1)S(1)} %fusion.3), channel_id=1, source_target_pairs={{0,8},{24,16},{1,9},{25,17},{2,10},{26,18},{3,11},{27,19},{4,12},{... | collective-permute-start | bytes 1228808 | tf_op jit(solution)/shard_map/ppermute | solution.py:821
  151.6 15.5 %collective-permute-start.32 = (bf16[320,640]{1,0:T(8,128)(2,1)S(1)}, bf16[320,640]{1,0:T(8,128)(2,1)S(1)}, u32[]{:S(2)}, u32[]{:S(2)}) collective-permute-start(bf16[320,640]{1,0:T(8,128)(2,1)S(1)} %fusion.2), channel_id=1, source_target_pairs={{0,8},{24,16},{1,9},{25,17},{2,10},{26,18},{3,11},{27,19},{4,12},{... | collective-permute-start | bytes 1228808 | tf_op jit(solution)/shard_map/ppermute | solution.py:821
  163.8 12.4 %collective-permute-start.37 = (bf16[80,2560]{1,0:T(8,128)(2,1)S(1)}, bf16[80,2560]{1,0:T(8,128)(2,1)S(1)}, u32[]{:S(2)}, u32[]{:S(2)}) collective-permute-start(bf16[80,2560]{1,0:T(8,128)(2,1)S(1)} %fusion.8), channel_id=1, source_target_pairs={{0,4},{1,5},{2,6},{3,7},{4,0},{5,1},{6,2},{7,3},{8,12},{9,13},{10,... | collective-permute-start | bytes 1228808 | tf_op jit(solution)/shard_map/ppermute | solution.py:785
  166.5 12.4 %collective-permute-start.38 = (bf16[80,2560]{1,0:T(8,128)(2,1)S(1)}, bf16[80,2560]{1,0:T(8,128)(2,1)S(1)}, u32[]{:S(2)}, u32[]{:S(2)}) collective-permute-start(bf16[80,2560]{1,0:T(8,128)(2,1)S(1)} %fusion.9), channel_id=1, source_target_pairs={{0,2},{1,3},{2,0},{3,1},{4,6},{5,7},{6,4},{7,5},{8,10},{9,11},{10,... | collective-permute-start | bytes 1228808 | tf_op jit(solution)/shard_map/ppermute | solution.py:785
  167.4 21.8 %collective-permute-start.41 = (bf16[640,640]{1,0:T(8,128)(2,1)S(1)}, bf16[640,640]{1,0:T(8,128)(2,1)S(1)}, u32[]{:S(2)}, u32[]{:S(2)}) collective-permute-start(bf16[640,640]{1,0:T(8,128)(2,1)S(1)} %pad_maximum_fusion), channel_id=1, source_target_pairs={{8,16},{16,8},{9,17},{17,9},{10,18},{18,10},{11,19},{19,11},{12,20... | collective-permute-start | bytes 2457608 | tf_op jit(solution)/shard_map/ppermute | solution.py:821
  169.0 18.9 %collective-permute-start.35 = (bf16[2,88,1280]{2,1,0:T(8,128)(2,1)S(1)}, bf16[2,88,1280]{2,1,0:T(8,128)(2,1)S(1)}, u32[]{:S(2)}, u32[]{:S(2)}) collective-permute-start(bf16[2,88,1280]{2,1,0:T(8,128)(2,1)S(1)} %get-tuple-element.223), channel_id=1, source_target_pairs={{0,2},{1,3},{2,0},{3,1},{4,6},{5,7},{6,4},{7,5},{8,10},{9,11},{10,... | collective-permute-start | bytes 1351688 | tf_op jit(solution)/shard_map/ppermute | solution.py:785
  170.5 17.3 %collective-permute-start.36 = (bf16[2,88,1280]{2,1,0:T(8,128)(2,1)S(1)}, bf16[2,88,1280]{2,1,0:T(8,128)(2,1)S(1)}, u32[]{:S(2)}, u32[]{:S(2)}) collective-permute-start(bf16[2,88,1280]{2,1,0:T(8,128)(2,1)S(1)} %get-tuple-element.222), channel_id=1, source_target_pairs={{0,4},{1,5},{2,6},{3,7},{4,0},{5,1},{6,2},{7,3},{8,12},{9,13},{10,... | collective-permute-start | bytes 1351688 | tf_op jit(solution)/shard_map/ppermute | solution.py:785
  181.2 16.6 %collective-permute-start.43 = (bf16[80,2560]{1,0:T(8,128)(2,1)S(1)}, bf16[80,2560]{1,0:T(8,128)(2,1)S(1)}, u32[]{:S(2)}, u32[]{:S(2)}) collective-permute-start(bf16[80,2560]{1,0:T(8,128)(2,1)S(1)} %fusion.1), channel_id=1, source_target_pairs={{0,8},{24,16},{1,9},{25,17},{2,10},{26,18},{3,11},{27,19},{4,12},{... | collective-permute-start | bytes 1228808 | tf_op jit(solution)/shard_map/ppermute | solution.py:821
  182.5 18.6 %collective-permute-start.45 = (bf16[80,2560]{1,0:T(8,128)(2,1)S(1)}, bf16[80,2560]{1,0:T(8,128)(2,1)S(1)}, u32[]{:S(2)}, u32[]{:S(2)}) collective-permute-start(bf16[80,2560]{1,0:T(8,128)(2,1)S(1)} %fusion), channel_id=1, source_target_pairs={{0,8},{24,16},{1,9},{25,17},{2,10},{26,18},{3,11},{27,19},{4,12},{... | collective-permute-start | bytes 1228808 | tf_op jit(solution)/shard_map/ppermute | solution.py:821
  189.4 22.8 %collective-permute-start.54 = (bf16[640,640]{1,0:T(8,128)(2,1)S(1)}, bf16[640,640]{1,0:T(8,128)(2,1)S(1)}, u32[]{:S(2)}, u32[]{:S(2)}) collective-permute-start(bf16[640,640]{1,0:T(8,128)(2,1)S(1)} %add_convert_fusion.1), channel_id=1, source_target_pairs={{8,0},{16,24},{9,1},{17,25},{10,2},{18,26},{11,3},{19,27},{12,4},{... | collective-permute-start | bytes 2457608 | tf_op jit(solution)/shard_map/ppermute | solution.py:821
  202.0 18.8 %collective-permute-start.52 = (bf16[80,2560]{1,0:T(8,128)(2,1)S(1)}, bf16[80,2560]{1,0:T(8,128)(2,1)S(1)}, u32[]{:S(2)}, u32[]{:S(2)}) collective-permute-start(bf16[80,2560]{1,0:T(8,128)(2,1)S(1)} %add_convert_fusion.3), channel_id=1, source_target_pairs={{8,0},{16,24},{9,1},{17,25},{10,2},{18,26},{11,3},{19,27},{12,4},{... | collective-permute-start | bytes 1228808 | tf_op jit(solution)/shard_map/ppermute | solution.py:821
  206.8 24.9 %collective-permute-start.53 = (bf16[80,2560]{1,0:T(8,128)(2,1)S(1)}, bf16[80,2560]{1,0:T(8,128)(2,1)S(1)}, u32[]{:S(2)}, u32[]{:S(2)}) collective-permute-start(bf16[80,2560]{1,0:T(8,128)(2,1)S(1)} %add_convert_fusion.2), channel_id=1, source_target_pairs={{8,0},{16,24},{9,1},{17,25},{10,2},{18,26},{11,3},{19,27},{12,4},{... | collective-permute-start | bytes 1228808 | tf_op jit(solution)/shard_map/ppermute | solution.py:821
  209.5 25.5 %collective-permute-start.50 = (bf16[88,1280]{1,0:T(8,128)(2,1)S(1)}, bf16[88,1280]{1,0:T(8,128)(2,1)S(1)}, u32[]{:S(2)}, u32[]{:S(2)}) collective-permute-start(bf16[88,1280]{1,0:T(8,128)(2,1)S(1)} %add_convert_fusion.13.refs_0_), channel_id=1, source_target_pairs={{8,0},{16,24},{9,1},{17,25},{10,2},{18,26},{11,3},{19,27},{12,4},{... | collective-permute-start | bytes 675848 | tf_op jit(solution)/shard_map/ppermute | solution.py:821
  210.9 26.6 %collective-permute-start.51 = (bf16[88,1280]{1,0:T(8,128)(2,1)S(1)}, bf16[88,1280]{1,0:T(8,128)(2,1)S(1)}, u32[]{:S(2)}, u32[]{:S(2)}) collective-permute-start(bf16[88,1280]{1,0:T(8,128)(2,1)S(1)} %add_convert_fusion.12.refs_1_), channel_id=1, source_target_pairs={{8,0},{16,24},{9,1},{17,25},{10,2},{18,26},{11,3},{19,27},{12,4},{... | collective-permute-start | bytes 675848 | tf_op jit(solution)/shard_map/ppermute | solution.py:821
  (67 other events, 564.2 us)

commit v2 on v1

--- a/solution.py
+++ b/solution.py
@@ -766,7 +766,7 @@
 
 def settle_kernel(rows, hidden, place_ref, *refs):
     totals, outers, refs = refs[:2], refs[2:4], refs[4:]
-    heads_ref, out_ref, short_ref, loss_ref, count_ref = refs
+    heads_ref, out_ref, up_ref, loss_ref, count_ref, *short_refs = refs
     width = out_ref.shape[1]
     inner = (place_ref[0] == 1) | (place_ref[0] == 2)
     left, right = [
@@ -775,7 +775,9 @@
     heads_ref[:, : 2 * width] = left[:rows]
     heads_ref[:, 2 * width :] = right[:rows, :width]
     out_ref[...] = right[:rows, width:]
-    short_ref[...] = left[rows:]
+    up_ref[...] = left[rows, LANES : LANES + hidden]
+    for at, ref in enumerate(short_refs):
+        ref[...] = left[rows + at, :rows]
     lanes = left[rows:, LANES + hidden : 2 * LANES + hidden]
     loss_ref[0] = jnp.sum(lanes[0:1])
     count_ref[0] = jnp.sum(lanes[1:2]).astype(jnp.int32)
@@ -1136,26 +1138,25 @@
         up_out = after(up_out, down_weight_sum, slab_out[0])
         upper, lower = [settle(*pair) for pair in zip(up_total, up_out)]
         first = core == 0
+        crossed = swap(jnp.where(first, lower, upper), 1)
         (up_weight_sum,) = call(
             functools.partial(join_kernel, hidden),
             [((rows, 2 * half), F32)],
-            (jnp.where(first, upper, lower), swap(jnp.where(first, lower, upper), 1)),
+            (jnp.where(first, upper, lower), crossed),
             core_position,
         )
-        slab_out = after(slab_out, upper, lower)
+        slab_out = after(slab_out, crossed)
         scalar = pl.BlockSpec(memory_space=pltpu.SMEM)
-        heads_sum, output_sum, short, loss_sum, token_count = call(
+        heads_sum, output_sum, up_bias_grad, loss_sum, token_count, *vectors_sum = call(
             functools.partial(settle_kernel, rows, hidden),
             [
-                ((rows, 3 * width), F32), ((rows, width), F32), ((VECTORS, 2 * width), F32),
-                ((1,), F32), ((1,), jnp.int32),
+                ((rows, 3 * width), F32), ((rows, width), F32), ((hidden,), F32),
+                ((1,), F32), ((1,), jnp.int32), *[((rows,), F32)] * VECTORS,
             ],
             (*slab_total, *slab_out),
             lax.axis_index("narrow").reshape(1).astype(jnp.int32),
-            out_specs=[vmem, vmem, vmem, scalar, scalar],
-        )
-        vectors_sum = short[:, :rows]
-        up_bias_grad = short[0, LANES : LANES + hidden]
+            out_specs=[vmem, vmem, vmem, scalar, scalar, *[vmem] * VECTORS],
+        )
         loss_sum, token_count = loss_sum.reshape(()), token_count.reshape(())
     else:
         down_weight_sum = collect_chips(down_parts[0].reshape(chips, hidden, width))

time: 242 us -> 246 us (1.017)
  waiting for transfers between devices: 88.7 us -> 93.9 us
    ppermute x16, waiting for transfers between devices: 29.5 us -> 34.6 us  [hop(): return [lax.ppermute(part, 'narrow', pairs) for part in parts]]
  transfers between devices with their start and end apart: 56 -> 56, of which waited for: 26 -> 27; matrix products, arithmetic and copies ran while one was open for 6% -> 5% of each run, Pallas kernels for 31% -> 30%
where the time goes in v2:
time: 246 us; the launch traced here: 245 us
  waiting for transfers between devices  93.9 us (38%)
  Pallas kernels  83.4 us (34%)
  starting transfers between devices  50.9 us (21%)
  other arithmetic  12.3 us (5%)
  local copies, waits for them, and re-layouts  2.66 us (1%)
    pallas_call x16, Pallas kernels, call(): pl.pallas_call(kernel, out_shape=shapes, grid_spec=pltpu.PrefetchScalarGr...  83.4 us
    ppermute x40, waiting for transfers between devices, swap(): lax.ppermute(values, 'wide', [(i, i ^ bit) for i in range(lax.axis_size('...  59.2 us
    ppermute x16, waiting for transfers between devices, hop(): return [lax.ppermute(part, 'narrow', pairs) for part in parts]  34.6 us
    ppermute x40, starting transfers between devices, swap(): lax.ppermute(values, 'wide', [(i, i ^ bit) for i in range(lax.axis_size('...  30.7 us
    ppermute x16, starting transfers between devices, hop(): return [lax.ppermute(part, 'narrow', pairs) for part in parts]  20.2 us
    convert_element_type x21, other arithmetic, add_low(): return sum((part.astype(F32) for part in parts)).astype(BF16)  10.8 us
  transfers between devices with their start and end apart: 56, of which 27 were waited for; matrix products, arithmetic and copies ran while one was open for 5% of the time, Pallas kernels for 30%

profile of v2, /device:TPU:0, one launch (start us, length us, event | category | flops | bytes accessed | tf_op | source)
XLA Modules:
  0.0 244.9 jit_solution(15713054716127511812)
XLA Ops:
  3.2 3.0 %collective-permute-start = (bf16[88,2560]{1,0:T(8,128)(2,1)S(1)}, bf16[88,2560]{1,0:T(8,128)(2,1)S(1)}, u32[]{:S(2)}, u32[]{:S(2)}) collective-permute-start(bf16[88,2560]{1,0:T(8,128)(2,1)S(1)} %shard_map.305.refs_0_), channel_id=1, source_target_pairs={{0,2},{1,3},{2,0},{3,1},{4,6},{5,7},{6,4},{7,5},{8,10},{9,11},{10,... | collective-permute-start | bytes 1351688 | tf_op jit(solution)/shard_map/ppermute | solution.py:787
  7.8 9.6 %collective-permute-done.refs_1_ = bf16[88,2560]{1,0:T(8,128)(2,1)S(1)} collective-permute-done((bf16[88,2560]{1,0:T(8,128)(2,1)S(1)}, bf16[88,2560]{1,0:T(8,128)(2,1)S(1)}, u32[]{:S(2)}, u32[]{:S(2)}) %collective-permute-start) | collective-permute-done | bytes 450592 | tf_op jit(solution)/shard_map/ppermute | solution.py:787
  17.5 2.1 collective-permute-start.7
  21.1 8.0 %collective-permute-done.2.refs_2_ = bf16[88,2560]{1,0:T(8,128)(2,1)S(1)} collective-permute-done((bf16[88,2560]{1,0:T(8,128)(2,1)S(1)}, bf16[88,2560]{1,0:T(8,128)(2,1)S(1)}, u32[]{:S(2)}, u32[]{:S(2)}) %collective-permute-start.2) | collective-permute-done | bytes 450592 | tf_op jit(solution)/shard_map/ppermute | solution.py:787
  32.4 5.2 %shard_map.306 = (bf16[512,640]{1,0:T(8,128)(2,1)S(1)}, bf16[512,1920]{1,0:T(8,128)(2,1)S(1)}, bf16[640,1920]{1,0:T(8,128)(2,1)S(1)}, bf16[640,640]{1,0:T(8,128)...) custom-call(s32[8]{0:T(128)S(1)} %pad_add_fusion.position_ref, bf16[512,640]{1,0:T(8,128)(2,1)} %bitcast.53, ...), custom_call_target="tpu_custom_call" | custom-call | flops 1 | bytes 1 | tf_op jit(solution)/shard_map/pallas_call | solution.py:56
  37.7 7.9 %shard_map.307 = (bf16[512,640]{1,0:T(8,128)(2,1)S(1)}, f32[640,512]{1,0:T(8,128)S(1)}, f32[40,512]{1,0:T(8,128)S(1)}) custom-call(s32[1,512]{1,0:T(1,128)S(1)} %copy-done.26, bf16[512,1920]{1,0:T(8,128)(2,1)S(1)} %get-tuple-element.126.q_ref.k_ref.v_ref, bf16[512,1920]{1,0:T(8,128)(2,1)S(1)} %get-tuple-element.126.q_ref.k_ref.v_ref, ...), custom_call_target="tpu_custom_call" | custom-call | flops 1 | bytes 1 | tf_op jit(solution)/shard_map/pallas_call | solution.py:56
  50.3 7.9 %collective-permute-done.13.refs_3_ = bf16[40,5120]{1,0:T(8,128)(2,1)S(1)} collective-permute-done((bf16[40,5120]{1,0:T(8,128)(2,1)S(1)}, bf16[40,5120]{1,0:T(8,128)(2,1)S(1)}, u32[]{:S(2)}, u32[]{:S(2)}) %collective-permute-start.13) | collective-permute-done | bytes 409632 | tf_op jit(solution)/shard_map/ppermute | solution.py:787
  62.8 9.5 %shard_map.309 = (bf16[1024,2560]{1,0:T(8,128)(2,1)S(1)}, bf16[1024,2560]{1,0:T(8,128)(2,1)S(1)}, bf16[640,2560]{1,0:T(8,128)(2,1)S(1)}) custom-call(s32[11]{0:T(128)S(1)} %compare_select_fusion.1.position_ref, bf16[512,640]{1,0:T(8,128)(2,1)S(1)} %get-tuple-element.136.own_ref.second_ref, ...), custom_call_target="tpu_custom_call" | custom-call | flops 1 | bytes 1 | tf_op jit(solution)/shard_map/pallas_call | solution.py:56
  75.3 4.5 %collective-permute-done.17.refs_1_ = bf16[320,640]{1,0:T(8,128)(2,1)S(1)} collective-permute-done((bf16[320,640]{1,0:T(8,128)(2,1)S(1)}, bf16[320,640]{1,0:T(8,128)(2,1)S(1)}, u32[]{:S(2)}, u32[]{:S(2)}) %collective-permute-start.17) | collective-permute-done | bytes 409632 | tf_op jit(solution)/shard_map/ppermute | solution.py:787
  81.1 4.4 %shard_map.310 = (f32[1024,640]{1,0:T(8,128)S(1)}, bf16[2560,640]{1,0:T(8,128)(2,1)S(1)}) custom-call(s32[7]{0:T(128)S(1)} %compare_select_fusion.2.position_ref, bf16[1024,2560]{1,0:T(8,128)(2,1)S(1)} %get-tuple-element.138.act_ref, bf16[640,640]{1,0:T(8,128)(2,1)S(1)} %copy-done.2, bf16[320,640]{1,0:T(8,128)(2,1)S(1)} %collective-permute-done.17.refs_1_, ...), custom_call_target="tpu_custom_call" | custom-call | flops 1 | bytes 1 | tf_op jit(solution)/shard_map/pallas_call | solution.py:56
  85.5 2.6 %collective-permute-done.21.upper_ref = bf16[320,640]{1,0:T(8,128)(2,1)S(1)} collective-permute-done((bf16[320,640]{1,0:T(8,128)(2,1)S(1)}, bf16[320,640]{1,0:T(8,128)(2,1)S(1)}, u32[]{:S(2)}, u32[]{:S(2)}) %collective-permute-start.21) | collective-permute-done | bytes 409632 | tf_op jit(solution)/shard_map/ppermute | solution.py:787
  89.2 1.9 shard_map.311
  91.1 2.1 collective-permute-done.23.got_ref
  94.5 2.0 collective-permute-done.24.other_ref
  96.5 4.3 %shard_map.313 = (bf16[2,320,640]{2,1,0:T(8,128)(2,1)S(1)}, bf16[2,320,640]{2,1,0:T(8,128)(2,1)S(1)}, bf16[2,320,640]{2,1,0:T(8,128)(2,1)S(1)}, bf16[2,320,640]{2,1,0:T(8,128)(2,1)S(1)}) custom-call(s32[1]{0:T(128)} %bitcast.11.position_ref, bf16[1024,2560]{1,0:T(8,128)(2,1)S(1)} %get-tuple-element.138.act_ref, ...), custom_call_target="tpu_custom_call" | custom-call | flops 1 | bytes 1 | tf_op jit(solution)/shard_map/pallas_call | solution.py:56
  102.9 10.9 %shard_map.314 = (bf16[1024,2560]{1,0:T(8,128)(2,1)S(1)}, f32[1,2560]{1,0:T(1,128)S(1)}, bf16[2,80,2560]{2,1,0:T(8,128)(2,1)S(1)}, bf16[2,80,2560]{2,1,0:T(8,128...) custom-call(s32[1]{0:T(128)} %bitcast.11.position_ref, ...), custom_call_target="tpu_custom_call" | custom-call | flops 1 | bytes 1 | tf_op jit(solution)/shard_map/pallas_call | solution.py:56
  113.8 6.0 %shard_map.315 = (f32[512,640]{1,0:T(8,128)}, bf16[512,640]{1,0:T(8,128)(2,1)}) custom-call(bf16[1024,2560]{1,0:T(8,128)(2,1)S(1)} %get-tuple-element.156.grad_ref, bf16[640,2560]{1,0:T(8,128)(2,1)S(1)} %get-tuple-element.157.up_ref), custom_call_target="tpu_custom_call" | custom-call | flops 1 | bytes 1 | tf_op jit(solution)/shard_map/pallas_call | solution.py:56
  127.2 5.1 %shard_map.316 = (f32[512,640]{1,0:T(8,128)S(1)}, bf16[512,640]{1,0:T(8,128)(2,1)S(1)}, bf16[512,640]{1,0:T(8,128)(2,1)S(1)}, f32[8,640]{1,0:T(8,128)S(1)}) custom-call(bf16[512,640]{1,0:T(8,128)(2,1)} %collective-permute-done.25.got_ref, f32[512,640]{1,0:T(8,128)} %get-tuple-element.163.own_far, f32[512,640]{1,0:T(8,128)} %copy-done.1, ...), custom_call_target="tpu_custom_call" | custom-call | flops 1 | bytes 1 | tf_op jit(solution)/shard_map/pallas_call | solution.py:56
  132.5 13.0 %shard_map.317 = (bf16[512,640]{1,0:T(8,128)(2,1)S(1)}, bf16[512,640]{1,0:T(8,128)(2,1)S(1)}, bf16[512,640]{1,0:T(8,128)(2,1)S(1)}) custom-call(s32[1,512]{1,0:T(1,128)S(1)} %copy-done.27, bf16[512,1920]{1,0:T(8,128)(2,1)S(1)} %get-tuple-element.126.q_ref.k_ref.v_ref, bf16[512,1920]{1,0:T(8,128)(2,1)S(1)} %get-tuple-element.126.q_ref.k_ref.v_ref, ...), custom_call_target="tpu_custom_call" | custom-call | flops 1 | bytes 1 | tf_op jit(solution)/shard_map/pallas_call | solution.py:56
  146.9 3.5 %collective-permute-start.31 = (bf16[320,640]{1,0:T(8,128)(2,1)S(1)}, bf16[320,640]{1,0:T(8,128)(2,1)S(1)}, u32[]{:S(2)}, u32[]{:S(2)}) collective-permute-start(bf16[320,640]{1,0:T(8,128)(2,1)S(1)} %fusion.3), channel_id=1, source_target_pairs={{0,8},{24,16},{1,9},{25,17},{2,10},{26,18},{3,11},{27,19},{4,12},{... | collective-permute-start | bytes 1228808 | tf_op jit(solution)/shard_map/ppermute | solution.py:823
  153.0 9.7 %shard_map.318 = (bf16[8,88,1280]{2,1,0:T(8,128)(2,1)S(1)}, bf16[8,88,1280]{2,1,0:T(8,128)(2,1)S(1)}, f32[512,640]{1,0:T(8,128)}, f32[8,640]{1,0:T(8,128)}, bf16[640,2560]{1,0:T(8,128)(2,1)}) custom-call(s32[8]{0:T(128)S(1)} %copy-done.31, bf16[512,640]{1,0:T(8,128)(2,1)S(1)} %bitcast.55, bf16[512,640]{1,0:T(8,128)(2,1)S(1)} %copy-done.20, ...), custom_call_target="tpu_custom_call" | custom-call | flops 1 | bytes 1 | tf_op jit(solution)/shard_map/pallas_call | solution.py:56
  163.8 1.6 collective-permute-start.37
  171.0 5.2 %collective-permute-done.37 = bf16[80,2560]{1,0:T(8,128)(2,1)S(1)} collective-permute-done((bf16[80,2560]{1,0:T(8,128)(2,1)S(1)}, bf16[80,2560]{1,0:T(8,128)(2,1)S(1)}, u32[]{:S(2)}, u32[]{:S(2)}) %collective-permute-start.37) | collective-permute-done | bytes 409632 | tf_op jit(solution)/shard_map/ppermute | solution.py:787
  176.2 2.7 %collective-permute-done.38 = bf16[80,2560]{1,0:T(8,128)(2,1)S(1)} collective-permute-done((bf16[80,2560]{1,0:T(8,128)(2,1)S(1)}, bf16[80,2560]{1,0:T(8,128)(2,1)S(1)}, u32[]{:S(2)}, u32[]{:S(2)}) %collective-permute-start.38) | collective-permute-done | bytes 409632 | tf_op jit(solution)/shard_map/ppermute | solution.py:787
  183.9 4.0 %collective-permute-done.35 = bf16[2,88,1280]{2,1,0:T(8,128)(2,1)S(1)} collective-permute-done((bf16[2,88,1280]{2,1,0:T(8,128)(2,1)S(1)}, bf16[2,88,1280]{2,1,0:T(8,128)(2,1)S(1)}, u32[]{:S(2)}, u32[]{:S(2)}) %collective-permute-start.35) | collective-permute-done | bytes 450592 | tf_op jit(solution)/shard_map/ppermute | solution.py:787
  190.7 4.1 %collective-permute-done.39 = bf16[88,1280]{1,0:T(8,128)(2,1)S(1)} collective-permute-done((bf16[88,1280]{1,0:T(8,128)(2,1)S(1)}, bf16[88,1280]{1,0:T(8,128)(2,1)S(1)}, u32[]{:S(2)}, u32[]{:S(2)}) %collective-permute-start.39) | collective-permute-done | bytes 225312 | tf_op jit(solution)/shard_map/ppermute | solution.py:787
  198.7 2.5 %collective-permute-done.45 = bf16[80,2560]{1,0:T(8,128)(2,1)S(1)} collective-permute-done((bf16[80,2560]{1,0:T(8,128)(2,1)S(1)}, bf16[80,2560]{1,0:T(8,128)(2,1)S(1)}, u32[]{:S(2)}, u32[]{:S(2)}) %collective-permute-start.45) | collective-permute-done | bytes 409632 | tf_op jit(solution)/shard_map/ppermute | solution.py:823
  203.3 2.6 %collective-permute-done.42 = bf16[88,1280]{1,0:T(8,128)(2,1)S(1)} collective-permute-done((bf16[88,1280]{1,0:T(8,128)(2,1)S(1)}, bf16[88,1280]{1,0:T(8,128)(2,1)S(1)}, u32[]{:S(2)}, u32[]{:S(2)}) %collective-permute-start.42) | collective-permute-done | bytes 225312 | tf_op jit(solution)/shard_map/ppermute | solution.py:823
  213.3 7.5 %collective-permute-done.52 = bf16[80,2560]{1,0:T(8,128)(2,1)S(1)} collective-permute-done((bf16[80,2560]{1,0:T(8,128)(2,1)S(1)}, bf16[80,2560]{1,0:T(8,128)(2,1)S(1)}, u32[]{:S(2)}, u32[]{:S(2)}) %collective-permute-start.52) | collective-permute-done | bytes 409632 | tf_op jit(solution)/shard_map/ppermute | solution.py:823
  220.8 9.4 %collective-permute-done.53 = bf16[80,2560]{1,0:T(8,128)(2,1)S(1)} collective-permute-done((bf16[80,2560]{1,0:T(8,128)(2,1)S(1)}, bf16[80,2560]{1,0:T(8,128)(2,1)S(1)}, u32[]{:S(2)}, u32[]{:S(2)}) %collective-permute-start.53) | collective-permute-done | bytes 409632 | tf_op jit(solution)/shard_map/ppermute | solution.py:823
  230.2 2.4 collective-permute-done.50.refs_2_
  234.1 8.5 %collective-permute-done.51.refs_3_ = bf16[88,1280]{1,0:T(8,128)(2,1)S(1)} collective-permute-done((bf16[88,1280]{1,0:T(8,128)(2,1)S(1)}, bf16[88,1280]{1,0:T(8,128)(2,1)S(1)}, u32[]{:S(2)}, u32[]{:S(2)}) %collective-permute-start.51) | collective-permute-done | bytes 225312 | tf_op jit(solution)/shard_map/ppermute | solution.py:823
  (216 shorter events, 69.7 us)
Async XLA Ops:
  3.2 14.2 %collective-permute-start = (bf16[88,2560]{1,0:T(8,128)(2,1)S(1)}, bf16[88,2560]{1,0:T(8,128)(2,1)S(1)}, u32[]{:S(2)}, u32[]{:S(2)}) collective-permute-start(bf16[88,2560]{1,0:T(8,128)(2,1)S(1)} %shard_map.305.refs_0_), channel_id=1, source_target_pairs={{0,2},{1,3},{2,0},{3,1},{4,6},{5,7},{6,4},{7,5},{8,10},{9,11},{10,... | collective-permute-start | bytes 1351688 | tf_op jit(solution)/shard_map/ppermute | solution.py:787
  6.2 22.9 %collective-permute-start.2 = (bf16[88,2560]{1,0:T(8,128)(2,1)S(1)}, bf16[88,2560]{1,0:T(8,128)(2,1)S(1)}, u32[]{:S(2)}, u32[]{:S(2)}) collective-permute-start(bf16[88,2560]{1,0:T(8,128)(2,1)S(1)} %shard_map.305.refs_0_), channel_id=1, source_target_pairs={{0,4},{1,5},{2,6},{3,7},{4,0},{5,1},{6,2},{7,3},{8,12},{9,13},{10,... | collective-permute-start | bytes 1351688 | tf_op jit(solution)/shard_map/ppermute | solution.py:787
  7.7 21.4 %collective-permute-start.3 = (bf16[88,2560]{1,0:T(8,128)(2,1)S(1)}, bf16[88,2560]{1,0:T(8,128)(2,1)S(1)}, u32[]{:S(2)}, u32[]{:S(2)}) collective-permute-start(bf16[88,2560]{1,0:T(8,128)(2,1)S(1)} %shard_map.305.refs_0_), channel_id=1, source_target_pairs={{0,6},{1,7},{2,4},{3,5},{4,2},{5,3},{6,0},{7,1},{8,14},{9,15},{10,... | collective-permute-start | bytes 1351688 | tf_op jit(solution)/shard_map/ppermute | solution.py:787
  17.5 28.2 %collective-permute-start.7 = (bf16[80,5120]{1,0:T(8,128)(2,1)}, bf16[80,5120]{1,0:T(8,128)(2,1)S(1)}, u32[]{:S(2)}, u32[]{:S(2)}) collective-permute-start(bf16[80,5120]{1,0:T(8,128)(2,1)} %refs_0_.1), channel_id=1, source_target_pairs={{0,2},{1,3},{2,0},{3,1},{4,6},{5,7},{6,4},{7,5},{8,10},{9,11},{10,... | collective-permute-start | bytes 2457608 | tf_op jit(solution)/shard_map/ppermute | solution.py:787
  19.5 26.6 %collective-permute-start.8 = (bf16[80,5120]{1,0:T(8,128)(2,1)}, bf16[80,5120]{1,0:T(8,128)(2,1)S(1)}, u32[]{:S(2)}, u32[]{:S(2)}) collective-permute-start(bf16[80,5120]{1,0:T(8,128)(2,1)} %refs_0_.1), channel_id=1, source_target_pairs={{0,4},{1,5},{2,6},{3,7},{4,0},{5,1},{6,2},{7,3},{8,12},{9,13},{10,... | collective-permute-start | bytes 2457608 | tf_op jit(solution)/shard_map/ppermute | solution.py:787
  29.7 20.4 %collective-permute-start.9 = (bf16[80,5120]{1,0:T(8,128)(2,1)}, bf16[80,5120]{1,0:T(8,128)(2,1)S(1)}, u32[]{:S(2)}, u32[]{:S(2)}) collective-permute-start(bf16[80,5120]{1,0:T(8,128)(2,1)} %refs_0_.1), channel_id=1, source_target_pairs={{0,1},{1,0},{2,3},{3,2},{4,5},{5,4},{6,7},{7,6},{8,9},{9,8},{10,11... | collective-permute-start | bytes 2457608 | tf_op jit(solution)/shard_map/ppermute | solution.py:787
  50.1 12.7 %collective-permute-start.12 = (bf16[512,640]{1,0:T(8,128)(2,1)S(1)}, bf16[512,640]{1,0:T(8,128)(2,1)S(1)}, u32[]{:S(2)}, u32[]{:S(2)}) collective-permute-start(bf16[512,640]{1,0:T(8,128)(2,1)S(1)} %get-tuple-element.136.own_ref.second_ref), channel_id=1, source_target_pairs={{0,1},{1,0},{2,3},{3,2},{4,5},{5,4},{6,7},{7,6},{8,9},{9,8},{10,11... | collective-permute-start | bytes 1966088 | tf_op jit(solution)/shard_map/ppermute | solution.py:787
  58.7 13.7 %collective-permute-start.18 = (bf16[320,640]{1,0:T(8,128)(2,1)S(1)}, bf16[320,640]{1,0:T(8,128)(2,1)S(1)}, u32[]{:S(2)}, u32[]{:S(2)}) collective-permute-start(bf16[320,640]{1,0:T(8,128)(2,1)S(1)} %get-tuple-element.140), channel_id=1, source_target_pairs={{0,2},{1,3},{2,0},{3,1},{4,6},{5,7},{6,4},{7,5},{8,10},{9,11},{10,... | collective-permute-start | bytes 1228808 | tf_op jit(solution)/shard_map/ppermute | solution.py:787
  60.0 12.4 %collective-permute-start.19 = (bf16[320,640]{1,0:T(8,128)(2,1)S(1)}, bf16[320,640]{1,0:T(8,128)(2,1)S(1)}, u32[]{:S(2)}, u32[]{:S(2)}) collective-permute-start(bf16[320,640]{1,0:T(8,128)(2,1)S(1)} %get-tuple-element.139), channel_id=1, source_target_pairs={{0,4},{1,5},{2,6},{3,7},{4,0},{5,1},{6,2},{7,3},{8,12},{9,13},{10,... | collective-permute-start | bytes 1228808 | tf_op jit(solution)/shard_map/ppermute | solution.py:787
  61.5 18.2 %collective-permute-start.17 = (bf16[320,640]{1,0:T(8,128)(2,1)S(1)}, bf16[320,640]{1,0:T(8,128)(2,1)S(1)}, u32[]{:S(2)}, u32[]{:S(2)}) collective-permute-start(bf16[320,640]{1,0:T(8,128)(2,1)S(1)} %get-tuple-element.139), channel_id=1, source_target_pairs={{0,2},{1,3},{2,0},{3,1},{4,6},{5,7},{6,4},{7,5},{8,10},{9,11},{10,... | collective-permute-start | bytes 1228808 | tf_op jit(solution)/shard_map/ppermute | solution.py:787
  62.3 18.8 %collective-permute-start.20 = (bf16[320,640]{1,0:T(8,128)(2,1)S(1)}, bf16[320,640]{1,0:T(8,128)(2,1)S(1)}, u32[]{:S(2)}, u32[]{:S(2)}) collective-permute-start(bf16[320,640]{1,0:T(8,128)(2,1)S(1)} %get-tuple-element.140), channel_id=1, source_target_pairs={{0,4},{1,5},{2,6},{3,7},{4,0},{5,1},{6,2},{7,3},{8,12},{9,13},{10,... | collective-permute-start | bytes 1228808 | tf_op jit(solution)/shard_map/ppermute | solution.py:787
  72.4 15.7 %collective-permute-start.21 = (bf16[320,640]{1,0:T(8,128)(2,1)S(1)}, bf16[320,640]{1,0:T(8,128)(2,1)S(1)}, u32[]{:S(2)}, u32[]{:S(2)}) collective-permute-start(bf16[320,640]{1,0:T(8,128)(2,1)S(1)} %collective-permute-done.19.refs_3_), channel_id=1, source_target_pairs={{0,2},{1,3},{2,0},{3,1},{4,6},{5,7},{6,4},{7,5},{8,10},{9,11},{10,... | collective-permute-start | bytes 1228808 | tf_op jit(solution)/shard_map/ppermute | solution.py:787
  73.8 15.4 %collective-permute-start.22 = (bf16[320,640]{1,0:T(8,128)(2,1)S(1)}, bf16[320,640]{1,0:T(8,128)(2,1)S(1)}, u32[]{:S(2)}, u32[]{:S(2)}) collective-permute-start(bf16[320,640]{1,0:T(8,128)(2,1)S(1)} %collective-permute-done.18.refs_2_), channel_id=1, source_target_pairs={{0,4},{1,5},{2,6},{3,7},{4,0},{5,1},{6,2},{7,3},{8,12},{9,13},{10,... | collective-permute-start | bytes 1228808 | tf_op jit(solution)/shard_map/ppermute | solution.py:787
  100.8 20.4 %collective-permute-start.26 = (bf16[2,320,640]{2,1,0:T(8,128)(2,1)S(1)}, bf16[2,320,640]{2,1,0:T(8,128)(2,1)S(1)}, u32[]{:S(2)}, u32[]{:S(2)}) collective-permute-start(bf16[2,320,640]{2,1,0:T(8,128)(2,1)S(1)} %get-tuple-element.152), channel_id=1, source_target_pairs={{0,2},{1,3},{2,0},{3,1},{4,6},{5,7},{6,4},{7,5},{8,10},{9,11},{10,... | collective-permute-start | bytes 2457608 | tf_op jit(solution)/shard_map/ppermute | solution.py:787
  101.5 22.1 %collective-permute-start.27 = (bf16[2,320,640]{2,1,0:T(8,128)(2,1)S(1)}, bf16[2,320,640]{2,1,0:T(8,128)(2,1)S(1)}, u32[]{:S(2)}, u32[]{:S(2)}) collective-permute-start(bf16[2,320,640]{2,1,0:T(8,128)(2,1)S(1)} %get-tuple-element.161), channel_id=1, source_target_pairs={{0,4},{1,5},{2,6},{3,7},{4,0},{5,1},{6,2},{7,3},{8,12},{9,13},{10,... | collective-permute-start | bytes 2457608 | tf_op jit(solution)/shard_map/ppermute | solution.py:787
  122.1 23.4 %collective-permute-start.28 = (bf16[320,640]{1,0:T(8,128)(2,1)}, bf16[320,640]{1,0:T(8,128)(2,1)}, u32[]{:S(2)}, u32[]{:S(2)}) collective-permute-start(bf16[320,640]{1,0:T(8,128)(2,1)} %fusion.6), channel_id=1, source_target_pairs={{0,4},{1,5},{2,6},{3,7},{4,0},{5,1},{6,2},{7,3},{8,12},{9,13},{10,... | collective-permute-start | bytes 1228808 | tf_op jit(solution)/shard_map/ppermute | solution.py:787
  124.7 20.9 %collective-permute-start.29 = (bf16[320,640]{1,0:T(8,128)(2,1)}, bf16[320,640]{1,0:T(8,128)(2,1)}, u32[]{:S(2)}, u32[]{:S(2)}) collective-permute-start(bf16[320,640]{1,0:T(8,128)(2,1)} %fusion.7), channel_id=1, source_target_pairs={{0,2},{1,3},{2,0},{3,1},{4,6},{5,7},{6,4},{7,5},{8,10},{9,11},{10,... | collective-permute-start | bytes 1228808 | tf_op jit(solution)/shard_map/ppermute | solution.py:787
  125.2 37.5 %collective-permute-start.33 = (bf16[2,80,2560]{2,1,0:T(8,128)(2,1)}, bf16[2,80,2560]{2,1,0:T(8,128)(2,1)}, u32[]{:S(2)}, u32[]{:S(2)}) collective-permute-start(bf16[2,80,2560]{2,1,0:T(8,128)(2,1)} %get-tuple-element.188), channel_id=1, source_target_pairs={{0,2},{1,3},{2,0},{3,1},{4,6},{5,7},{6,4},{7,5},{8,10},{9,11},{10,... | collective-permute-start | bytes 2457608 | tf_op jit(solution)/shard_map/ppermute | solution.py:787
  126.7 36.0 %collective-permute-start.34 = (bf16[2,80,2560]{2,1,0:T(8,128)(2,1)}, bf16[2,80,2560]{2,1,0:T(8,128)(2,1)}, u32[]{:S(2)}, u32[]{:S(2)}) collective-permute-start(bf16[2,80,2560]{2,1,0:T(8,128)(2,1)} %get-tuple-element.189), channel_id=1, source_target_pairs={{0,4},{1,5},{2,6},{3,7},{4,0},{5,1},{6,2},{7,3},{8,12},{9,13},{10,... | collective-permute-start | bytes 2457608 | tf_op jit(solution)/shard_map/ppermute | solution.py:787
  146.9 20.2 %collective-permute-start.31 = (bf16[320,640]{1,0:T(8,128)(2,1)S(1)}, bf16[320,640]{1,0:T(8,128)(2,1)S(1)}, u32[]{:S(2)}, u32[]{:S(2)}) collective-permute-start(bf16[320,640]{1,0:T(8,128)(2,1)S(1)} %fusion.3), channel_id=1, source_target_pairs={{0,8},{24,16},{1,9},{25,17},{2,10},{26,18},{3,11},{27,19},{4,12},{... | collective-permute-start | bytes 1228808 | tf_op jit(solution)/shard_map/ppermute | solution.py:823
  151.6 15.5 %collective-permute-start.32 = (bf16[320,640]{1,0:T(8,128)(2,1)S(1)}, bf16[320,640]{1,0:T(8,128)(2,1)S(1)}, u32[]{:S(2)}, u32[]{:S(2)}) collective-permute-start(bf16[320,640]{1,0:T(8,128)(2,1)S(1)} %fusion.2), channel_id=1, source_target_pairs={{0,8},{24,16},{1,9},{25,17},{2,10},{26,18},{3,11},{27,19},{4,12},{... | collective-permute-start | bytes 1228808 | tf_op jit(solution)/shard_map/ppermute | solution.py:823
  163.8 12.4 %collective-permute-start.37 = (bf16[80,2560]{1,0:T(8,128)(2,1)S(1)}, bf16[80,2560]{1,0:T(8,128)(2,1)S(1)}, u32[]{:S(2)}, u32[]{:S(2)}) collective-permute-start(bf16[80,2560]{1,0:T(8,128)(2,1)S(1)} %fusion.8), channel_id=1, source_target_pairs={{0,4},{1,5},{2,6},{3,7},{4,0},{5,1},{6,2},{7,3},{8,12},{9,13},{10,... | collective-permute-start | bytes 1228808 | tf_op jit(solution)/shard_map/ppermute | solution.py:787
  166.5 12.4 %collective-permute-start.38 = (bf16[80,2560]{1,0:T(8,128)(2,1)S(1)}, bf16[80,2560]{1,0:T(8,128)(2,1)S(1)}, u32[]{:S(2)}, u32[]{:S(2)}) collective-permute-start(bf16[80,2560]{1,0:T(8,128)(2,1)S(1)} %fusion.9), channel_id=1, source_target_pairs={{0,2},{1,3},{2,0},{3,1},{4,6},{5,7},{6,4},{7,5},{8,10},{9,11},{10,... | collective-permute-start | bytes 1228808 | tf_op jit(solution)/shard_map/ppermute | solution.py:787
  167.4 21.8 %collective-permute-start.41 = (bf16[640,640]{1,0:T(8,128)(2,1)S(1)}, bf16[640,640]{1,0:T(8,128)(2,1)S(1)}, u32[]{:S(2)}, u32[]{:S(2)}) collective-permute-start(bf16[640,640]{1,0:T(8,128)(2,1)S(1)} %pad_maximum_fusion), channel_id=1, source_target_pairs={{8,16},{16,8},{9,17},{17,9},{10,18},{18,10},{11,19},{19,11},{12,20... | collective-permute-start | bytes 2457608 | tf_op jit(solution)/shard_map/ppermute | solution.py:823
  169.0 18.9 %collective-permute-start.35 = (bf16[2,88,1280]{2,1,0:T(8,128)(2,1)S(1)}, bf16[2,88,1280]{2,1,0:T(8,128)(2,1)S(1)}, u32[]{:S(2)}, u32[]{:S(2)}) collective-permute-start(bf16[2,88,1280]{2,1,0:T(8,128)(2,1)S(1)} %get-tuple-element.236), channel_id=1, source_target_pairs={{0,2},{1,3},{2,0},{3,1},{4,6},{5,7},{6,4},{7,5},{8,10},{9,11},{10,... | collective-permute-start | bytes 1351688 | tf_op jit(solution)/shard_map/ppermute | solution.py:787
  170.5 17.3 %collective-permute-start.36 = (bf16[2,88,1280]{2,1,0:T(8,128)(2,1)S(1)}, bf16[2,88,1280]{2,1,0:T(8,128)(2,1)S(1)}, u32[]{:S(2)}, u32[]{:S(2)}) collective-permute-start(bf16[2,88,1280]{2,1,0:T(8,128)(2,1)S(1)} %get-tuple-element.235), channel_id=1, source_target_pairs={{0,4},{1,5},{2,6},{3,7},{4,0},{5,1},{6,2},{7,3},{8,12},{9,13},{10,... | collective-permute-start | bytes 1351688 | tf_op jit(solution)/shard_map/ppermute | solution.py:787
  181.2 16.6 %collective-permute-start.43 = (bf16[80,2560]{1,0:T(8,128)(2,1)S(1)}, bf16[80,2560]{1,0:T(8,128)(2,1)S(1)}, u32[]{:S(2)}, u32[]{:S(2)}) collective-permute-start(bf16[80,2560]{1,0:T(8,128)(2,1)S(1)} %fusion.1), channel_id=1, source_target_pairs={{0,8},{24,16},{1,9},{25,17},{2,10},{26,18},{3,11},{27,19},{4,12},{... | collective-permute-start | bytes 1228808 | tf_op jit(solution)/shard_map/ppermute | solution.py:823
  182.5 18.6 %collective-permute-start.45 = (bf16[80,2560]{1,0:T(8,128)(2,1)S(1)}, bf16[80,2560]{1,0:T(8,128)(2,1)S(1)}, u32[]{:S(2)}, u32[]{:S(2)}) collective-permute-start(bf16[80,2560]{1,0:T(8,128)(2,1)S(1)} %fusion), channel_id=1, source_target_pairs={{0,8},{24,16},{1,9},{25,17},{2,10},{26,18},{3,11},{27,19},{4,12},{... | collective-permute-start | bytes 1228808 | tf_op jit(solution)/shard_map/ppermute | solution.py:823
  189.4 22.6 %collective-permute-start.54 = (bf16[640,640]{1,0:T(8,128)(2,1)S(1)}, bf16[640,640]{1,0:T(8,128)(2,1)S(1)}, u32[]{:S(2)}, u32[]{:S(2)}) collective-permute-start(bf16[640,640]{1,0:T(8,128)(2,1)S(1)} %add_convert_fusion.1), channel_id=1, source_target_pairs={{8,0},{16,24},{9,1},{17,25},{10,2},{18,26},{11,3},{19,27},{12,4},{... | collective-permute-start | bytes 2457608 | tf_op jit(solution)/shard_map/ppermute | solution.py:823
  202.0 18.8 %collective-permute-start.52 = (bf16[80,2560]{1,0:T(8,128)(2,1)S(1)}, bf16[80,2560]{1,0:T(8,128)(2,1)S(1)}, u32[]{:S(2)}, u32[]{:S(2)}) collective-permute-start(bf16[80,2560]{1,0:T(8,128)(2,1)S(1)} %add_convert_fusion.3), channel_id=1, source_target_pairs={{8,0},{16,24},{9,1},{17,25},{10,2},{18,26},{11,3},{19,27},{12,4},{... | collective-permute-start | bytes 1228808 | tf_op jit(solution)/shard_map/ppermute | solution.py:823
  206.8 23.4 %collective-permute-start.53 = (bf16[80,2560]{1,0:T(8,128)(2,1)S(1)}, bf16[80,2560]{1,0:T(8,128)(2,1)S(1)}, u32[]{:S(2)}, u32[]{:S(2)}) collective-permute-start(bf16[80,2560]{1,0:T(8,128)(2,1)S(1)} %add_convert_fusion.2), channel_id=1, source_target_pairs={{8,0},{16,24},{9,1},{17,25},{10,2},{18,26},{11,3},{19,27},{12,4},{... | collective-permute-start | bytes 1228808 | tf_op jit(solution)/shard_map/ppermute | solution.py:823
  209.5 23.1 %collective-permute-start.50 = (bf16[88,1280]{1,0:T(8,128)(2,1)S(1)}, bf16[88,1280]{1,0:T(8,128)(2,1)S(1)}, u32[]{:S(2)}, u32[]{:S(2)}) collective-permute-start(bf16[88,1280]{1,0:T(8,128)(2,1)S(1)} %add_convert_fusion.13.refs_0_), channel_id=1, source_target_pairs={{8,0},{16,24},{9,1},{17,25},{10,2},{18,26},{11,3},{19,27},{12,4},{... | collective-permute-start | bytes 675848 | tf_op jit(solution)/shard_map/ppermute | solution.py:823
  (67 other events, 567.0 us)
